TPU v7x, 32 devices: a whole 2x2x4 slice. The times are simulated.
32 devices in a mesh: cohort: 4 (over x, core), fsdp: 8 (over z, y).
Axes of the slice: x: 2, y: 2, z: 4, core: 2. Of those that a mesh axis runs over, the one named last changes fastest.
Arguments:
- client_tokens: bfloat16 [4, 4, 2, 64, 3584], P('cohort', None, None, 'fsdp'), may hold values from -18 to 18
- targets: bfloat16 [4, 4, 2, 64, 7168], P('cohort', None, None, None, 'fsdp'), may hold values from -12 to 12
- weights: bfloat16 [7168, 3584], P('fsdp'), may hold values from -6 to 6
- momentum: float32 [7168, 3584], P('fsdp', 'cohort'), may hold values from -2 to 2
- noise_now: bfloat16 [7168, 3584], P('fsdp', 'cohort'), may hold values from -6 to 6
- noise_prev: bfloat16 [7168, 3584], P('fsdp', 'cohort'), may hold values from -6 to 6
Outputs:
- new_weights: bfloat16 [7168, 3584], P('fsdp')
- new_momentum: float32 [7168, 3584], P('fsdp', 'cohort')
All inputs are finite; a program needn't handle non-finite values.
Results may differ from a plain program's by a relative error of at most 0.0028.
The roundings to bfloat16 on the way count: a program that leaves them out, or rounds other values in their place, can miss the bound.
Values may be sent and summed in bfloat16 or wider, within the bound.
A program may use at most 128 MiB of HBM per device.

v0:
```python
import math

import jax
import jax.numpy as jnp
from jax import lax
from jax.sharding import PartitionSpec as P

D = 3584
CLIENTS = 4
STEPS = 2


LOCAL_LR = 300.0
CLIP_BOUND = 32.0
NOISE_STD = 0.0004
BAND_COEF = 0.5
MOMENTUM_DECAY = 0.9
SERVER_LR = 0.5
EPSILON = 1e-06


def gelu_parts(preact):
    inner = 0.7978845608 * (preact + 0.044715 * preact * preact * preact)
    tangent = jnp.tanh(inner)
    activation = 0.5 * preact * (1.0 + tangent)
    slope = 0.5 * (1.0 + tangent) + 0.5 * preact * (1.0 - tangent * tangent) * 0.7978845608 * (
        1.0 + 3.0 * 0.044715 * preact * preact
    )
    return (activation, slope)


def clip_factor(squared):
    return jnp.minimum(1.0, CLIP_BOUND / (jnp.sqrt(squared) + EPSILON))


def local_update(token_block, target_block, current, client_delta):
    token_count = token_block.shape[0]
    preact = lax.dot_general(
        token_block, current, (((1,), (1,)), ((), ())), preferred_element_type=jnp.float32
    ) * (1.0 / math.sqrt(D))
    activation, slope = gelu_parts(preact)
    error_term = ((activation - target_block.astype(jnp.float32)) * slope).astype(jnp.bfloat16)
    gradient = lax.dot_general(
        error_term, token_block, (((0,), (0,)), ((), ())), preferred_element_type=jnp.float32
    )
    return client_delta - LOCAL_LR / (token_count * math.sqrt(D)) * gradient


def body(client_tokens, targets, weights, momentum, noise_now, noise_prev):
    base_weights = weights.astype(jnp.float32)
    round_block = lax.all_gather(client_tokens[0], "fsdp", axis=2, tiled=True)
    cohort_sum = jnp.zeros(base_weights.shape, jnp.float32)
    for client_index in range(CLIENTS):
        client_delta = jnp.zeros(base_weights.shape, jnp.float32)
        current = weights
        for step_index in range(STEPS):
            token_block = round_block[client_index, step_index]
            client_delta = local_update(
                token_block, targets[0, client_index, step_index], current, client_delta
            )
            if step_index + 1 < STEPS:
                current = (base_weights + client_delta).astype(jnp.bfloat16)
        squared = lax.psum(jnp.sum(client_delta * client_delta), "fsdp")
        cohort_sum = cohort_sum + clip_factor(squared) * client_delta
    totals = lax.psum_scatter(cohort_sum, "cohort", scatter_dimension=1, tiled=True)
    owner_width = totals.shape[1]
    owner_start = lax.axis_index("cohort") * owner_width
    base_part = lax.dynamic_slice_in_dim(base_weights, owner_start, owner_width, 1)
    cohort_count = lax.axis_size("cohort")
    hidden_count = weights.shape[0] * lax.axis_size("fsdp")
    noise = (
        NOISE_STD
        * CLIP_BOUND
        * (noise_now.astype(jnp.float32) - BAND_COEF * noise_prev.astype(jnp.float32))
    )
    aggregate = (
        math.sqrt(hidden_count * D) / (cohort_count * CLIENTS * CLIP_BOUND) * (totals + noise)
    )
    new_momentum = MOMENTUM_DECAY * momentum + aggregate
    new_part = (base_part + SERVER_LR * new_momentum).astype(jnp.bfloat16)
    new_weights = lax.all_gather(new_part, "cohort", axis=1, tiled=True)
    return (new_weights, new_momentum)


def solution(mesh):
    in_specs = (
        P("cohort", None, None, "fsdp", None),
        P("cohort", None, None, None, "fsdp"),
        P("fsdp", None),
        P("fsdp", "cohort"),
        P("fsdp", "cohort"),
        P("fsdp", "cohort"),
    )
    out_specs = (P("fsdp", None), P("fsdp", "cohort"))
    return jax.shard_map(body, mesh=mesh, in_specs=in_specs, out_specs=out_specs, check_vma=False)
```

profile of v0, /device:TPU:0, one launch (start us, length us, event | category | flops | bytes accessed | tf_op | source)
XLA Modules:
  0.0 416.9 jit_solution(12804104453435907457)
XLA Ops:
  7.2 0.0 all-gather.6.cloned.1.call-start
  7.2 0.7 all-gather.6.cloned.1.call-update
  7.9 0.0 reduce-scatter.2.cloned.1.call-start
  7.9 71.2 %all-gather.6.cloned.1.call-done = bf16[1,4,2,64,3584]{4,3,2,1,0:T(8,128)(2,1)} async-done(((bf16[1,4,2,8,3584]{4,3,2,1,0:T(8,128)(2,1)}), bf16[1,4,2,64,3584]{4,3,2,1,0:T(8,128)(2,1)}) %all-gather.6.cloned.1.call-update) | async-done | bytes 3670032 | tf_op jit(solution)/shard_map/all_gather | solution.py:51
  79.1 11.9 %fusion.8 = f32[896,3584]{1,0:T(8,128)} fusion(bf16[4,2,64,3584]{3,2,1,0:T(8,128)(2,1)} %bitcast.317, bf16[896,3584]{1,0:T(8,128)(2,1)} %param.8, bf16[1,4,2,64,896]{4,3,2,1,0:T(8,128)(2,1)} %param.7), kind=kOutput, calls=%fused_computation.35 | convolution fusion | flops 823402496 | bytes 20299776 | tf_op jit(solution)/shard_map/dot_general | solution.py:43
  91.1 0.0 copy-done.1
  91.1 12.0 %fusion.6 = f32[896,3584]{1,0:T(8,128)} fusion(bf16[4,2,64,3584]{3,2,1,0:T(8,128)(2,1)} %bitcast.318, bf16[896,3584]{1,0:T(8,128)(2,1)} %param.8, bf16[1,4,2,64,896]{4,3,2,1,0:T(8,128)(2,1)S(1)} %copy-done.1), kind=kOutput, calls=%fused_computation.33 | convolution fusion | flops 823402496 | bytes 20299776 | tf_op jit(solution)/shard_map/dot_general | solution.py:43
  103.0 11.8 %fusion.4 = f32[896,3584]{1,0:T(8,128)} fusion(bf16[4,2,64,3584]{3,2,1,0:T(8,128)(2,1)} %bitcast.319, bf16[896,3584]{1,0:T(8,128)(2,1)} %param.8, bf16[1,4,2,64,896]{4,3,2,1,0:T(8,128)(2,1)S(1)} %copy-done.1), kind=kOutput, calls=%fused_computation.31 | convolution fusion | flops 823402496 | bytes 20299776 | tf_op jit(solution)/shard_map/dot_general | solution.py:43
  114.9 11.9 %fusion.10 = f32[896,3584]{1,0:T(8,128)} fusion(bf16[4,2,64,3584]{3,2,1,0:T(8,128)(2,1)} %bitcast.320, bf16[896,3584]{1,0:T(8,128)(2,1)} %param.8, bf16[1,4,2,64,896]{4,3,2,1,0:T(8,128)(2,1)S(1)} %copy-done.1), kind=kOutput, calls=%fused_computation.37 | convolution fusion | flops 823402496 | bytes 20299776 | tf_op jit(solution)/shard_map/dot_general | solution.py:43
  126.8 20.6 %multiply_reduce_fusion.1 = (f32[]{:T(128)}, f32[896,3584]{1,0:T(8,128)}) fusion(bf16[4,2,64,3584]{3,2,1,0:T(8,128)(2,1)} %bitcast.321, bf16[896,3584]{1,0:T(8,128)(2,1)} %param.8, f32[896,3584]{1,0:T(8,128)} %fusion.8, bf16[1,4,2,64,896]{4,3,2,1,0:T(8,128)(2,1)S(1)} %copy-done.1), kind=kOutput, calls=%fused_computation.5 | convolution fusion | flops 858726400 | bytes 45989892 | tf_op jit(solution)/shard_map/dot_general | solution.py:43
  147.3 20.4 %multiply_reduce_fusion.2 = (f32[]{:T(128)}, f32[896,3584]{1,0:T(8,128)}) fusion(bf16[4,2,64,3584]{3,2,1,0:T(8,128)(2,1)} %bitcast.322, bf16[896,3584]{1,0:T(8,128)(2,1)} %param.8, f32[896,3584]{1,0:T(8,128)} %fusion.6, bf16[1,4,2,64,896]{4,3,2,1,0:T(8,128)(2,1)S(1)} %copy-done.1), kind=kOutput, calls=%fused_computation.9 | convolution fusion | flops 858726400 | bytes 45989892 | tf_op jit(solution)/shard_map/dot_general | solution.py:43
  167.8 20.6 %multiply_reduce_fusion.3 = (f32[]{:T(128)}, f32[896,3584]{1,0:T(8,128)}) fusion(bf16[4,2,64,3584]{3,2,1,0:T(8,128)(2,1)} %bitcast.323, bf16[896,3584]{1,0:T(8,128)(2,1)} %param.8, f32[896,3584]{1,0:T(8,128)} %fusion.4, bf16[1,4,2,64,896]{4,3,2,1,0:T(8,128)(2,1)S(1)} %copy-done.1), kind=kOutput, calls=%fused_computation.13 | convolution fusion | flops 858726400 | bytes 45989892 | tf_op jit(solution)/shard_map/dot_general | solution.py:43
  188.4 20.5 %multiply_reduce_fusion = (f32[]{:T(128)}, f32[896,3584]{1,0:T(8,128)}) fusion(bf16[4,2,64,3584]{3,2,1,0:T(8,128)(2,1)} %bitcast.324, bf16[896,3584]{1,0:T(8,128)(2,1)} %param.8, f32[896,3584]{1,0:T(8,128)} %fusion.10, bf16[1,4,2,64,896]{4,3,2,1,0:T(8,128)(2,1)S(1)} %copy-done.1), kind=kOutput, calls=%fused_computation.1 | convolution fusion | flops 858726400 | bytes 45989892 | tf_op jit(solution)/shard_map/dot_general | solution.py:43
  208.8 19.8 %all-reduce = (f32[]{:T(128)}, f32[]{:T(128)}, f32[]{:T(128)}, f32[]{:T(128)}) all-reduce(f32[]{:T(128)} %get-tuple-element.8, f32[]{:T(128)} %get-tuple-element.10, f32[]{:T(128)} %get-tuple-element.12, f32[]{:T(128)} %get-tuple-element.14), channel_id=1, replica_groups=mesh['cohort'=4,'fsdp'=8] {'fsdp'}, use_global_device_ids=true, to_apply=%region_7.0 | all-reduce | flops 4 | bytes 32 | tf_op jit(solution)/shard_map/psum | solution.py:63
  231.4 22.4 %multiply_add_fusion = f32[896,3584]{1,0:T(8,128)} fusion(f32[896,3584]{1,0:T(8,128)} %get-tuple-element.9, f32[896,3584]{1,0:T(8,128)} %get-tuple-element.11, f32[896,3584]{1,0:T(8,128)} %get-tuple-element.13, f32[896,3584]{1,0:T(8,128)} %get-tuple-element.15, f32[]{:T(128)S(6)} %min.15, f32[]{:T(128)S(6)} %min.14, f32[]{:T(128)S(6)} %min.13, f32[]{:T(128)S(6)} %min.12), kind=kLoop, calls=%fused_computation | loop fusion | flops 22478848 | bytes 64225296 | tf_op jit(solution)/shard_map/add | solution.py:64
  253.8 0.0 reduce-scatter.2.cloned.1.call-update
  253.8 0.3 all-gather.4.cloned.1.call-start
  254.1 0.0 copy-start
  254.1 14.3 %convert_element_type.96 = f32[896,3584]{1,0:T(8,128)} convert(bf16[896,3584]{1,0:T(8,128)(2,1)} %param.8) | non-fusion elementwise | flops 3211264 | bytes 19267584 | tf_op jit(solution)/shard_map/convert_element_type | solution.py:50
  268.4 81.5 %reduce-scatter.2.cloned.1.call-done = f32[896,896]{1,0:T(8,128)} async-done(((f32[896,3584]{1,0:T(8,128)}), f32[896,896]{1,0:T(8,128)}) %reduce-scatter.2.cloned.1.call-update) | async-done | bytes 3211280 | tf_op jit(solution)/shard_map/reduce_scatter | solution.py:65
  350.0 7.2 %add_convert_fusion.8 = (bf16[896,896]{1,0:T(8,128)(2,1)}, f32[896,896]{1,0:T(8,128)}) fusion(f32[896,3584]{1,0:T(8,128)} %convert_element_type.96, s32[]{:T(128)S(6)} %select_n.3, f32[896,896]{1,0:T(8,128)} %reduce-scatter.2.cloned.1.call-done, bf16[896,896]{1,0:T(8,128)(2,1)} %param.11, bf16[896,896]{1,0:T(8,128)(2,1)} %param.10, f32[896,896]{1,0:T(8,128)S(1)} %copy-done), kind=kLoop, calls=%fused_computation.21 | loop fusion | flops 9633792 | bytes 17661956 | tf_op jit(solution)/shard_map/convert_element_type | solution.py:80
  357.2 0.0 all-gather.4.cloned.1.call-update
  357.2 47.2 %all-gather.4.cloned.1.call-done = bf16[896,3584]{1,0:T(8,128)(2,1)} async-done(((bf16[896,896]{1,0:T(8,128)(2,1)}), bf16[896,3584]{1,0:T(8,128)(2,1)}) %all-gather.4.cloned.1.call-update) | async-done | bytes 6422544 | tf_op jit(solution)/shard_map/all_gather | solution.py:81
  404.4 6.0 %copy.9 = bf16[896,3584]{1,0:T(8,128)(2,1)} copy(bf16[896,3584]{1,0:T(8,128)(2,1)} %all-gather.4.cloned.1.call-done) | data formatting | bytes 12845056
  (2 shorter events, 0.0 us)
Async XLA Ops:
  7.2 72.0 %all-gather.6.cloned.1.call-start = ((), (), s32[]{:S(2)}) async-start(), calls=%async_computation.3 | async-start | bytes 4128768 | tf_op jit(solution)/shard_map/all_gather | solution.py:51
  7.9 342.1 %reduce-scatter.2.cloned.1.call-start = ((), (), s32[]{:S(2)}) async-start(), calls=%async_computation.1 | async-start | bytes 16056320 | tf_op jit(solution)/shard_map/reduce_scatter | solution.py:65
  79.1 11.9 %copy-start.1 = (bf16[1,4,2,64,896]{4,3,2,1,0:T(8,128)(2,1)S(1)}, bf16[1,4,2,64,896]{4,3,2,1,0:T(8,128)(2,1)}, u32[]{:S(2)}) copy-start(bf16[1,4,2,64,896]{4,3,2,1,0:T(8,128)(2,1)} %param.7) | copy-start | bytes 2752516
  253.8 150.6 %all-gather.4.cloned.1.call-start = ((), (), s32[]{:S(2)}) async-start(), calls=%async_computation.2 | async-start | bytes 8028160 | tf_op jit(solution)/shard_map/all_gather | solution.py:81
  254.1 95.8 %copy-start = (f32[896,896]{1,0:T(8,128)S(1)}, f32[896,896]{1,0:T(8,128)}, u32[]{:S(2)}) copy-start(f32[896,896]{1,0:T(8,128)} %param.9) | copy-start | bytes 9633796
Sparse Core Ops, SparseCore 0:
  10.2 68.9 all-gather.5
  253.9 95.9 reduce-scatter.1
  357.3 47.0 all-gather.3
where the time goes:
time: 417 us
  waiting for transfers between devices  201 us (48%)
  matrix products  130 us (31%)
  other arithmetic  43.9 us (11%)
  blocking collectives  19.8 us (5%)
  between operations  16.5 us (4%)
  local copies, waits for them, and re-layouts  5.99 us (1%)
    dot_general x8, matrix products, local_update(): lax.dot_general(error_term, token_block, (((0,), (0,)), ((), ())), prefer...  130 us
    reduce_scatter x1, waiting for transfers between devices, body(): lax.psum_scatter(cohort_sum, 'cohort', scatter_dimension=1, tiled=True)  81.5 us
    all_gather x1, waiting for transfers between devices, body(): round_block = lax.all_gather(client_tokens[0], 'fsdp', axis=2, tiled=True)  71.2 us
    all_gather x1, waiting for transfers between devices, body(): new_weights = lax.all_gather(new_part, 'cohort', axis=1, tiled=True)  47.2 us
    add x1, other arithmetic, body(): cohort_sum = cohort_sum + clip_factor(squared) * client_delta  22.4 us
    psum x1, blocking collectives, body(): squared = lax.psum(jnp.sum(client_delta * client_delta), 'fsdp')  19.8 us
    convert_element_type x1, other arithmetic, body(): base_weights = weights.astype(jnp.float32)  14.3 us
  transfers between devices with their start and end apart: 3, of which 3 were waited for; matrix products, arithmetic and copies ran while one was open for 3% of the time, Pallas kernels for 0%

commit v1 on v0

v1 whole, which is shorter than its diff:
```python
import math

import jax
import jax.numpy as jnp
from jax import lax
from jax.sharding import PartitionSpec as P

LOCAL_LR = 300.0
CLIP_BOUND = 32.0
NOISE_STD = 0.0004
BAND_COEF = 0.5
MOMENTUM_DECAY = 0.9
SERVER_LR = 0.5
EPSILON = 1e-06


def gelu_parts(preact):
    inner = 0.7978845608 * (preact + 0.044715 * preact * preact * preact)
    tangent = jnp.tanh(inner)
    activation = 0.5 * preact * (1.0 + tangent)
    slope = 0.5 * (1.0 + tangent) + 0.5 * preact * (1.0 - tangent * tangent) * 0.7978845608 * (
        1.0 + 3.0 * 0.044715 * preact * preact
    )
    return (activation, slope)


def clip_factor(squared):
    return jnp.minimum(1.0, CLIP_BOUND / (jnp.sqrt(squared) + EPSILON))


def errors_of(preact, targets):
    activation, slope = gelu_parts(preact)
    return ((activation - targets.astype(jnp.float32)) * slope).astype(jnp.bfloat16)


def client_errors(tokens, targets, weights):
    clients, steps, count, depth = tokens.shape
    rate = LOCAL_LR / (count * math.sqrt(depth))
    scale = 1.0 / math.sqrt(depth)
    flat = tokens.reshape(clients, steps * count, depth)
    products = lax.dot_general(
        flat.reshape(clients * steps * count, depth),
        weights,
        (((1,), (1,)), ((), ())),
        preferred_element_type=jnp.float32,
    ).reshape(clients, steps, count, weights.shape[0])
    gram = jnp.einsum("ksd,ktd->kst", flat, flat, preferred_element_type=jnp.float32)
    errors = []
    for step in range(steps):
        preact = products[:, step]
        if step > 0:
            earlier = jnp.concatenate(errors, axis=1).astype(jnp.float32)
            cross = gram[:, step * count : (step + 1) * count, : step * count]
            preact = preact - rate * jnp.einsum(
                "kst,ktf->ksf", cross, earlier, precision=lax.Precision.HIGHEST
            )
        errors.append(errors_of(preact * scale, targets[:, step]))
    errors = jnp.concatenate(errors, axis=1)
    error_gram = jnp.einsum("ksf,ktf->kst", errors, errors, preferred_element_type=jnp.float32)
    squared = rate * rate * jnp.maximum(jnp.sum(error_gram * gram, axis=(1, 2)), 0.0)
    return errors, squared, rate


def weighted_sum(errors, factors, tokens):
    clients, count, hidden = errors.shape
    scaled = errors.astype(jnp.float32) * factors[:, None, None]
    high = scaled.astype(jnp.bfloat16)
    low = (scaled - high.astype(jnp.float32)).astype(jnp.bfloat16)
    tokens = tokens.reshape(clients * count, -1)
    dims = (((0,), (0,)), ((), ()))
    return sum(
        lax.dot_general(
            part.reshape(clients * count, hidden), tokens, dims, preferred_element_type=jnp.float32
        )
        for part in (high, low)
    )


def body(client_tokens, targets, weights, momentum, noise_now, noise_prev):
    depth = weights.shape[1]
    clients = client_tokens.shape[1]
    round_block = lax.all_gather(client_tokens[0], "fsdp", axis=2, tiled=True)
    errors, squared, rate = client_errors(round_block, targets[0], weights)
    squared = lax.psum(squared, "fsdp")
    cohort_sum = weighted_sum(errors, -rate * clip_factor(squared), round_block)
    totals = lax.psum_scatter(cohort_sum, "cohort", scatter_dimension=1, tiled=True)
    owner_width = totals.shape[1]
    owner_start = lax.axis_index("cohort") * owner_width
    base_part = lax.dynamic_slice_in_dim(weights, owner_start, owner_width, 1).astype(jnp.float32)
    cohort_count = lax.axis_size("cohort")
    hidden_count = weights.shape[0] * lax.axis_size("fsdp")
    noise = (
        NOISE_STD
        * CLIP_BOUND
        * (noise_now.astype(jnp.float32) - BAND_COEF * noise_prev.astype(jnp.float32))
    )
    aggregate = (
        math.sqrt(hidden_count * depth) / (cohort_count * clients * CLIP_BOUND) * (totals + noise)
    )
    new_momentum = MOMENTUM_DECAY * momentum + aggregate
    new_part = (base_part + SERVER_LR * new_momentum).astype(jnp.bfloat16)
    new_weights = lax.all_gather(new_part, "cohort", axis=1, tiled=True)
    return (new_weights, new_momentum)


def solution(mesh):
    in_specs = (
        P("cohort", None, None, "fsdp", None),
        P("cohort", None, None, None, "fsdp"),
        P("fsdp", None),
        P("fsdp", "cohort"),
        P("fsdp", "cohort"),
        P("fsdp", "cohort"),
    )
    out_specs = (P("fsdp", None), P("fsdp", "cohort"))
    return jax.shard_map(body, mesh=mesh, in_specs=in_specs, out_specs=out_specs, check_vma=False)
```

time: 417 us -> 289 us (0.69)
  matrix products: 130 us -> 26.6 us
  other arithmetic: 43.9 us -> 7.99 us
  waiting for transfers between devices: 201 us -> 214 us
    dot_general x8 -> x6, matrix products: 130 us -> 26.6 us  [the longest x2 12.5 us: weighted_sum(): lax.dot_general(part.reshape(clients * count, hidden), tokens, dims, pref...]
    add x1 -> x0, other arithmetic: 22.4 us -> none  [body(): cohort_sum = cohort_sum + clip_factor(squared) * client_delta]
    reduce_scatter x1, waiting for transfers between devices: 81.5 us -> 96.1 us  [body(): lax.psum_scatter(cohort_sum, 'cohort', scatter_dimension=1, tiled=True)]
    convert_element_type x1 -> x2, other arithmetic: 14.3 us -> 1.1 us  [the longest x1 0.71 us: errors_of(): ((activation - targets.astype(jnp.float32)) * slope).astype(jnp.bfloat16)]
  transfers between devices with their start and end apart: 3 -> 3, of which waited for: 3 -> 3; matrix products, arithmetic and copies ran while one was open for 3% -> 0% of each run, Pallas kernels for 0% -> 0%
where the time goes in v1:
time: 289 us
  waiting for transfers between devices  214 us (74%)
  matrix products  26.6 us (9%)
  blocking collectives  19.2 us (7%)
  between operations  13.8 us (5%)
  other arithmetic  7.99 us (3%)
  local copies, waits for them, and re-layouts  7.25 us (3%)
    reduce_scatter x1, waiting for transfers between devices, body(): lax.psum_scatter(cohort_sum, 'cohort', scatter_dimension=1, tiled=True)  96.1 us
    all_gather x1, waiting for transfers between devices, body(): round_block = lax.all_gather(client_tokens[0], 'fsdp', axis=2, tiled=True)  69.9 us
    all_gather x1, waiting for transfers between devices, body(): new_weights = lax.all_gather(new_part, 'cohort', axis=1, tiled=True)  47.2 us
    psum x1, blocking collectives, body(): squared = lax.psum(squared, 'fsdp')  19.2 us
    dot_general x2, matrix products, weighted_sum(): lax.dot_general(part.reshape(clients * count, hidden), tokens, dims, pref...  12.5 us
    dot_general x1, matrix products, client_errors(): lax.dot_general(flat.reshape(clients * steps * count, depth), weights, ((...  7.91 us
    unnamed x8, local copies, waits for them, and re-layouts  7.25 us
    convert_element_type x1, other arithmetic, body(): new_part = (base_part + SERVER_LR * new_momentum).astype(jnp.bfloat16)  6.87 us
  transfers between devices with their start and end apart: 3, of which 3 were waited for; matrix products, arithmetic and copies ran while one was open for 0% of the time, Pallas kernels for 0%

profile of v1, /device:TPU:0, one launch (start us, length us, event | category | flops | bytes accessed | tf_op | source)
XLA Modules:
  0.0 288.9 jit_solution(6339048571634710617)
XLA Ops:
  7.2 0.0 all-gather.6.cloned.1.call-start
  7.2 0.7 all-gather.6.cloned.1.call-update
  7.9 0.0 reduce-scatter.2.cloned.1.call-start
  7.9 1.3 copy.13
  9.2 69.9 %all-gather.6.cloned.1.call-done = bf16[1,4,2,64,3584]{4,3,2,1,0:T(8,128)(2,1)} async-done(((bf16[1,4,2,8,3584]{4,3,2,1,0:T(8,128)(2,1)}), bf16[1,4,2,64,3584]{4,3,2,1,0:T(8,128)(2,1)}) %all-gather.6.cloned.1.call-update) | async-done | bytes 3670032 | tf_op jit(solution)/shard_map/all_gather | solution.py:82
  79.1 4.4 %fusion.20 = f32[4,128,128]{2,1,0:T(8,128)S(1)} fusion(bf16[4,128,3584]{2,1,0:T(8,128)(2,1)} %bitcast.70), kind=kOutput, calls=%fused_computation.42 | convolution fusion | flops 469762048 | bytes 3932160 | tf_op jit(solution)/shard_map/ksd,ktd->kst/dot_general | solution.py:47
  83.5 0.0 copy-done
  83.6 7.9 %fusion = f32[4,2,64,896]{3,2,1,0:T(8,128)S(1)} fusion(bf16[896,3584]{1,0:T(8,128)(2,1)} %param.8, bf16[1,4,2,64,3584]{4,3,2,1,0:T(8,128)(2,1)S(1)} %copy-done), kind=kOutput, calls=%fused_computation.1 | convolution fusion | flops 3288334336 | bytes 11927552 | tf_op jit(solution)/shard_map/dot_general | solution.py:41
  91.5 0.7 fusion.13
  92.2 1.2 fusion.11
  93.4 0.5 fusion.5
  94.0 19.2 %psum.7 = f32[4]{0:T(128)S(1)} all-reduce(f32[4]{0:T(128)S(1)} %maximum_multiply_fusion), channel_id=1, replica_groups=mesh['cohort'=4,'fsdp'=8] {'fsdp'}, use_global_device_ids=true, to_apply=%region_1.0 | all-reduce | flops 4 | bytes 32 | tf_op jit(solution)/shard_map/psum | solution.py:84
  113.1 0.4 subtract_convert_fusion
  113.5 0.0 copy-start.1
  113.5 5.7 %fusion.21 = f32[896,3584]{1,0:T(8,128)S(1)} fusion(bf16[512,896]{1,0:T(8,128)(2,1)S(1)} %bitcast.74, bf16[512,3584]{1,0:T(8,128)(2,1)} %bitcast.71), kind=kOutput, calls=%fused_computation.43 | convolution fusion | flops 3288334336 | bytes 17432576 | tf_op jit(solution)/shard_map/dot_general | solution.py:72
  119.3 0.0 copy-done.1
  119.3 6.8 %convolution_add_fusion = f32[896,3584]{1,0:T(8,128)} fusion(f32[896,3584]{1,0:T(8,128)S(1)} %fusion.21, bf16[512,896]{1,0:T(8,128)(2,1)S(1)} %bitcast.73, bf16[512,3584]{1,0:T(8,128)(2,1)S(1)} %bitcast.72), kind=kOutput, calls=%fused_computation | convolution fusion | flops 3291545600 | bytes 30277632 | tf_op jit(solution)/shard_map/dot_general | solution.py:72
  126.1 0.0 reduce-scatter.2.cloned.1.call-update
  126.1 0.0 all-gather.4.cloned.1.call-start
  126.2 96.1 %reduce-scatter.2.cloned.1.call-done = f32[896,896]{1,0:T(8,128)} async-done(((f32[896,3584]{1,0:T(8,128)}), f32[896,896]{1,0:T(8,128)}) %reduce-scatter.2.cloned.1.call-update) | async-done | bytes 3211280 | tf_op jit(solution)/shard_map/reduce_scatter | solution.py:86
  222.3 6.9 %add_convert_fusion = (bf16[896,896]{1,0:T(8,128)(2,1)}, f32[896,896]{1,0:T(8,128)}) fusion(bf16[896,3584]{1,0:T(8,128)(2,1)} %param.8, s32[]{:T(128)S(6)} %select_n.3, f32[896,896]{1,0:T(8,128)} %reduce-scatter.2.cloned.1.call-done, bf16[896,896]{1,0:T(8,128)(2,1)} %param.11, bf16[896,896]{1,0:T(8,128)(2,1)} %param.10, f32[896,896]{1,0:T(8,128)S(1)} %copy-done.2), kind=kLoop, calls=%fused_computation.4 | loop fusion | flops 10436608 | bytes 16056324 | tf_op jit(solution)/shard_map/convert_element_type | solution.py:101
  229.1 0.0 all-gather.4.cloned.1.call-update
  229.2 47.2 %all-gather.4.cloned.1.call-done = bf16[896,3584]{1,0:T(8,128)(2,1)} async-done(((bf16[896,896]{1,0:T(8,128)(2,1)}), bf16[896,3584]{1,0:T(8,128)(2,1)}) %all-gather.4.cloned.1.call-update) | async-done | bytes 6422544 | tf_op jit(solution)/shard_map/all_gather | solution.py:102
  276.4 6.0 %copy.15 = bf16[896,3584]{1,0:T(8,128)(2,1)} copy(bf16[896,3584]{1,0:T(8,128)(2,1)} %all-gather.4.cloned.1.call-done) | data formatting | bytes 12845056
  (5 shorter events, 0.0 us)
Async XLA Ops:
  7.2 72.0 %all-gather.6.cloned.1.call-start = ((), (), s32[]{:S(2)}) async-start(), calls=%async_computation.3 | async-start | bytes 4128768 | tf_op jit(solution)/shard_map/all_gather | solution.py:82
  7.9 214.4 %reduce-scatter.2.cloned.1.call-start = ((), (), s32[]{:S(2)}) async-start(), calls=%async_computation.1 | async-start | bytes 16056320 | tf_op jit(solution)/shard_map/reduce_scatter | solution.py:86
  79.1 4.4 %copy-start = (bf16[1,4,2,64,3584]{4,3,2,1,0:T(8,128)(2,1)S(1)}, bf16[1,4,2,64,3584]{4,3,2,1,0:T(8,128)(2,1)}, u32[]{:S(2)}) copy-start(bf16[1,4,2,64,3584]{4,3,2,1,0:T(8,128)(2,1)} %all-gather.6.cloned.1.call-done) | copy-start | bytes 11010052
  113.5 5.7 %copy-start.1 = (bf16[1,4,2,64,3584]{4,3,2,1,0:T(8,128)(2,1)S(1)}, bf16[1,4,2,64,3584]{4,3,2,1,0:T(8,128)(2,1)}, u32[]{:S(2)}) copy-start(bf16[1,4,2,64,3584]{4,3,2,1,0:T(8,128)(2,1)} %all-gather.6.cloned.1.call-done) | copy-start | bytes 11010052
  126.1 96.2 %copy-start.2 = (f32[896,896]{1,0:T(8,128)S(1)}, f32[896,896]{1,0:T(8,128)}, u32[]{:S(2)}) copy-start(f32[896,896]{1,0:T(8,128)} %param.9) | copy-start | bytes 9633796
  126.1 150.3 %all-gather.4.cloned.1.call-start = ((), (), s32[]{:S(2)}) async-start(), calls=%async_computation.2 | async-start | bytes 8028160 | tf_op jit(solution)/shard_map/all_gather | solution.py:102
Sparse Core Ops, SparseCore 0:
  10.2 68.9 all-gather.5
  126.2 95.9 reduce-scatter.1
  229.3 47.0 all-gather.3

commit v2 on v1

--- a/solution.py
+++ b/solution.py
@@ -3,6 +3,8 @@
 import jax
 import jax.numpy as jnp
 from jax import lax
+from jax.experimental import pallas as pl
+from jax.experimental.pallas import tpu as pltpu
 from jax.sharding import PartitionSpec as P
 
 LOCAL_LR = 300.0
@@ -31,6 +33,347 @@
 def errors_of(preact, targets):
     activation, slope = gelu_parts(preact)
     return ((activation - targets.astype(jnp.float32)) * slope).astype(jnp.bfloat16)
+
+
+MESH = pl.DeviceIdType.MESH
+ANY = pl.BlockSpec(memory_space=pl.ANY)
+IN_VMEM = pl.BlockSpec(memory_space=pltpu.VMEM)
+DMA = pltpu.SemaphoreType.DMA
+
+
+def remote(source, target, send, receive, cohort, fsdp):
+    return pltpu.make_async_remote_copy(
+        src_ref=source,
+        dst_ref=target,
+        send_sem=send,
+        recv_sem=receive,
+        device_id={"cohort": cohort, "fsdp": fsdp},
+        device_id_type=MESH,
+    )
+
+
+def signal(cohort, fsdp):
+    pl.semaphore_signal(
+        pltpu.get_barrier_semaphore(),
+        inc=1,
+        device_id={"cohort": cohort, "fsdp": fsdp},
+        device_id_type=MESH,
+    )
+
+
+def gather_kernel(
+    cohorts, shards, own_ref, all_ref, cut_ref, got, got_cut, to_up, to_down, to_pair, to_cut, kept, kept_cut
+):
+    c, f = lax.axis_index("cohort"), lax.axis_index("fsdp")
+    rows = shards // 2
+    row, side = f // 2, f % 2
+    pair = f + 1 - 2 * side
+    width = cut_ref.shape[-1]
+    others = [(c + j) % cohorts for j in range(1, cohorts)]
+
+    signal(c, (f + 2) % shards)
+    signal(c, (f + shards - 2) % shards)
+    signal(c, pair)
+    for other in others:
+        signal(other, f)
+    pl.semaphore_wait(pltpu.get_barrier_semaphore(), cohorts + 2)
+
+    def up(slot, source):
+        return remote(source, all_ref.at[slot], to_up.at[slot], got.at[slot], c, f + 2)
+
+    def down(slot, source):
+        return remote(source, all_ref.at[slot], to_down.at[slot], got.at[slot], c, f - 2)
+
+    def across(slot, source):
+        return remote(source, all_ref.at[slot], to_pair.at[slot], got.at[slot], c, pair)
+
+    def columns(source, owner):
+        return source.at[:, pl.ds(pl.multiple_of(owner * width, 128), width)]
+
+    def cuts(slot, source):
+        copies = [
+            remote(
+                columns(source, other),
+                cut_ref.at[c, slot],
+                to_cut.at[at, slot],
+                got_cut.at[c, slot],
+                other,
+                f,
+            )
+            for at, other in enumerate(others)
+        ]
+        own = pltpu.make_async_copy(columns(source, c), cut_ref.at[c, slot], kept_cut.at[slot])
+        return copies + [own]
+
+    def arrived(slot):
+        remote(
+            all_ref.at[slot], all_ref.at[slot], to_pair.at[slot], got.at[slot], c, pair
+        ).wait_recv()
+
+    def start(copies):
+        for copy in copies:
+            copy.start()
+
+    keep = pltpu.make_async_copy(own_ref, all_ref.at[f], kept)
+
+    @pl.when(row + 1 < rows)
+    def _():
+        up(f, own_ref).start()
+
+    @pl.when(row > 0)
+    def _():
+        down(f, own_ref).start()
+
+    across(f, own_ref).start()
+    start(cuts(f, own_ref))
+    keep.start()
+
+    for step in range(1, rows + 1):
+
+        @pl.when(row >= step)
+        def _():
+            slot = f - 2 * step
+            arrived(slot)
+
+            @pl.when(row + 1 < rows)
+            def _():
+                up(slot, all_ref.at[slot]).start()
+
+            across(slot, all_ref.at[slot]).start()
+            start(cuts(slot, all_ref.at[slot]))
+
+        @pl.when(row + step < rows)
+        def _():
+            slot = f + 2 * step
+            arrived(slot)
+
+            @pl.when(row > 0)
+            def _():
+                down(slot, all_ref.at[slot]).start()
+
+            across(slot, all_ref.at[slot]).start()
+            start(cuts(slot, all_ref.at[slot]))
+
+        last = step - 1
+
+        @pl.when(row >= last)
+        def _():
+            slot = pair - 2 * last
+            arrived(slot)
+            start(cuts(slot, all_ref.at[slot]))
+
+        if last > 0:
+
+            @pl.when(row + last < rows)
+            def _():
+                slot = pair + 2 * last
+                arrived(slot)
+                start(cuts(slot, all_ref.at[slot]))
+
+    keep.wait()
+    for line in range(rows):
+        slot = 2 * line + side
+
+        @pl.when((row + 1 < rows) & (line <= row))
+        def _():
+            up(slot, own_ref).wait_send()
+
+        @pl.when((row > 0) & (line >= row))
+        def _():
+            down(slot, own_ref).wait_send()
+
+        across(slot, own_ref).wait_send()
+    for slot in range(shards):
+        *sent, own = cuts(slot, own_ref)
+        own.wait()
+        for copy in sent:
+            copy.wait_send()
+        for other in others:
+            remote(
+                cut_ref.at[other, slot],
+                cut_ref.at[other, slot],
+                to_pair.at[slot],
+                got_cut.at[other, slot],
+                other,
+                f,
+            ).wait_recv()
+
+
+def gather_tokens(tokens, cohorts, shards):
+    count, depth = tokens.shape
+    return pl.pallas_call(
+        lambda *refs: gather_kernel(cohorts, shards, *refs),
+        name="gather_tokens",
+        out_shape=(
+            jax.ShapeDtypeStruct((shards, count, depth), tokens.dtype),
+            jax.ShapeDtypeStruct((cohorts, shards, count, depth // cohorts), tokens.dtype),
+        ),
+        in_specs=[IN_VMEM],
+        out_specs=(IN_VMEM, ANY),
+        scratch_shapes=[
+            DMA((shards,)),
+            DMA((cohorts, shards)),
+            DMA((shards,)),
+            DMA((shards,)),
+            DMA((shards,)),
+            DMA((cohorts - 1, shards)),
+            DMA,
+            DMA((shards,)),
+        ],
+        compiler_params=pltpu.CompilerParams(
+            collective_id=0, has_side_effects=True, vmem_limit_bytes=60 << 20
+        ),
+    )(tokens)
+
+
+def spread_kernel(cohorts, own_ref, all_ref, got, to_far, to_pair, kept):
+    c, f = lax.axis_index("cohort"), lax.axis_index("fsdp")
+    pair = c + 1 - 2 * (c % 2)
+    pieces = own_ref.shape[0]
+    far = [(c + 2 * j) % cohorts for j in range(1, cohorts // 2)]
+    keep = pltpu.make_async_copy(own_ref, all_ref.at[c], kept)
+    keep.start()
+
+    def outward(at, piece):
+        return remote(
+            own_ref.at[piece],
+            all_ref.at[c, piece],
+            to_far.at[at, piece],
+            got.at[c, piece],
+            far[at],
+            f,
+        )
+
+    def across(slot, piece, source):
+        return remote(
+            source, all_ref.at[slot, piece], to_pair.at[slot, piece], got.at[slot, piece], pair, f
+        )
+
+    for piece in range(pieces):
+        for at in range(len(far)):
+            outward(at, piece).start()
+    for piece in range(pieces):
+        across(c, piece, own_ref.at[piece]).start()
+    for piece in range(pieces):
+        for slot in far:
+            copy = across(slot, piece, all_ref.at[slot, piece])
+            copy.wait_recv()
+            copy.start()
+    for piece in range(pieces):
+        for at in range(len(far)):
+            outward(at, piece).wait_send()
+        for slot in [c] + far:
+            across(slot, piece, own_ref.at[piece]).wait_send()
+        for j in range(cohorts // 2):
+            slot = (pair + 2 * j) % cohorts
+            across(slot, piece, own_ref.at[piece]).wait_recv()
+    keep.wait()
+
+
+def greet(cohorts, c, f, others):
+    signal(c + 1 - 2 * (c % 2), f)
+    for j in range(1, cohorts // 2):
+        signal((c + 2 * j) % cohorts, f)
+    for other in others:
+        signal(c, other)
+    pl.semaphore_wait(pltpu.get_barrier_semaphore(), cohorts // 2 + len(others))
+
+
+def blocks_kernel(cohorts, own_ref, all_ref, got, to_far, to_pair, kept):
+    greet(cohorts, lax.axis_index("cohort"), lax.axis_index("fsdp"), [])
+    spread_kernel(cohorts, own_ref, all_ref, got, to_far, to_pair, kept)
+
+
+def spread_blocks(block, cohorts, collective_id):
+    pieces = block.shape[0]
+    return pl.pallas_call(
+        lambda *refs: blocks_kernel(cohorts, *refs),
+        name="spread_blocks",
+        out_shape=jax.ShapeDtypeStruct((cohorts,) + block.shape, block.dtype),
+        in_specs=[IN_VMEM],
+        out_specs=ANY,
+        scratch_shapes=[
+            DMA((cohorts, pieces)),
+            DMA((max(cohorts // 2 - 1, 1), pieces)),
+            DMA((cohorts, pieces)),
+            DMA,
+        ],
+        compiler_params=pltpu.CompilerParams(
+            collective_id=collective_id, has_side_effects=True, vmem_limit_bytes=60 << 20
+        ),
+    )(block)
+
+
+def errors_kernel(
+    cohorts, shards, own_ref, part_ref, all_ref, norm_ref,
+    got, to_far, to_pair, kept, parts, total, got_part, to_part, got_norm, to_norm,
+):
+    c, f = lax.axis_index("cohort"), lax.axis_index("fsdp")
+    others = [(f + j) % shards for j in range(1, shards)]
+    cohort_others = [(c + j) % cohorts for j in range(1, cohorts)]
+    barrier = pltpu.get_barrier_semaphore()
+    for other in others:
+        signal(c, other)
+    for other in cohort_others:
+        signal(other, f)
+    pl.semaphore_wait(barrier, len(others) + len(cohort_others))
+
+    def part(at, source):
+        return remote(part_ref, parts.at[source], to_part.at[at], got_part.at[source], c, others[at])
+
+    def norm(at, source):
+        return remote(
+            total, norm_ref.at[source], to_norm.at[at], got_norm.at[source], cohort_others[at], f
+        )
+
+    for at in range(len(others)):
+        part(at, f).start()
+    parts[pl.ds(f, 1)] = part_ref[...][None]
+    for at, other in enumerate(others):
+        part(at, other).wait_recv()
+    summed = parts[0]
+    for at in range(1, shards):
+        summed = summed + parts[at]
+    total[...] = summed
+    norm_ref[pl.ds(c, 1)] = summed[None]
+    for at in range(len(cohort_others)):
+        norm(at, c).start()
+    spread_kernel(cohorts, own_ref, all_ref, got, to_far, to_pair, kept)
+    for at, other in enumerate(cohort_others):
+        norm(at, other).wait_recv()
+        norm(at, c).wait_send()
+    for at in range(len(others)):
+        part(at, f).wait_send()
+
+
+def spread_errors(errors, squared, cohorts, shards):
+    pieces = errors.shape[0]
+    tile = jnp.broadcast_to(squared[:, None], (squared.shape[0], 128))
+    return pl.pallas_call(
+        lambda *refs: errors_kernel(cohorts, shards, *refs),
+        name="spread_errors",
+        out_shape=(
+            jax.ShapeDtypeStruct((cohorts,) + errors.shape, errors.dtype),
+            jax.ShapeDtypeStruct((cohorts,) + tile.shape, tile.dtype),
+        ),
+        in_specs=[IN_VMEM, IN_VMEM],
+        out_specs=(ANY, IN_VMEM),
+        scratch_shapes=[
+            DMA((cohorts, pieces)),
+            DMA((max(cohorts // 2 - 1, 1), pieces)),
+            DMA((cohorts, pieces)),
+            DMA,
+            pltpu.VMEM((shards,) + tile.shape, tile.dtype),
+            pltpu.VMEM(tile.shape, tile.dtype),
+            DMA((shards,)),
+            DMA((shards,)),
+            DMA((cohorts,)),
+            DMA((cohorts,)),
+        ],
+        compiler_params=pltpu.CompilerParams(
+            collective_id=1, has_side_effects=True, vmem_limit_bytes=60 << 20
+        ),
+    )(errors, tile)
 
 
 def client_errors(tokens, targets, weights):
@@ -62,27 +405,63 @@
 
 
 def weighted_sum(errors, factors, tokens):
-    clients, count, hidden = errors.shape
-    scaled = errors.astype(jnp.float32) * factors[:, None, None]
+    hidden, width = errors.shape[-1], tokens.shape[-1]
+    scaled = errors.astype(jnp.float32) * factors
     high = scaled.astype(jnp.bfloat16)
     low = (scaled - high.astype(jnp.float32)).astype(jnp.bfloat16)
-    tokens = tokens.reshape(clients * count, -1)
+    tokens = tokens.reshape(-1, width)
     dims = (((0,), (0,)), ((), ()))
     return sum(
         lax.dot_general(
-            part.reshape(clients * count, hidden), tokens, dims, preferred_element_type=jnp.float32
+            part.reshape(-1, hidden), tokens, dims, preferred_element_type=jnp.float32
         )
         for part in (high, low)
     )
 
 
-def body(client_tokens, targets, weights, momentum, noise_now, noise_prev):
+def factor_body(client_tokens, targets, weights, momentum, noise_now, noise_prev):
+    cohorts, shards = lax.axis_size("cohort"), lax.axis_size("fsdp")
+    hidden, depth = weights.shape
+    _, clients, steps, count, _ = client_tokens.shape
+    gathered, columns = gather_tokens(client_tokens.reshape(-1, depth), cohorts, shards)
+    tokens = gathered.reshape(shards, clients, steps, count, depth)
+    tokens = tokens.transpose(1, 2, 0, 3, 4).reshape(clients, steps, shards * count, depth)
+    errors, squared, rate = client_errors(tokens, targets[0], weights)
+    errors = errors.reshape(clients, steps, shards, count, hidden).transpose(2, 0, 1, 3, 4)
+    errors, squared = spread_errors(errors.reshape(shards, -1, hidden), squared, cohorts, shards)
+    factors = -rate * clip_factor(squared[:, :, 0])
+    errors = errors.reshape(cohorts, shards, clients, steps * count, hidden)
+    totals = weighted_sum(errors, factors[:, None, :, None, None], columns)
+    owner_width = totals.shape[1]
+    owner_start = lax.axis_index("cohort") * owner_width
+    base_part = lax.dynamic_slice_in_dim(weights, owner_start, owner_width, 1).astype(jnp.float32)
+    hidden_count = hidden * shards
+    noise = (
+        NOISE_STD
+        * CLIP_BOUND
+        * (noise_now.astype(jnp.float32) - BAND_COEF * noise_prev.astype(jnp.float32))
+    )
+    aggregate = (
+        math.sqrt(hidden_count * depth) / (cohorts * clients * CLIP_BOUND) * (totals + noise)
+    )
+    new_momentum = MOMENTUM_DECAY * momentum + aggregate
+    new_part = (base_part + SERVER_LR * new_momentum).astype(jnp.bfloat16)
+    pieces = math.gcd(hidden // 16, 8)
+    new_part = new_part.reshape(pieces, hidden // pieces, owner_width)
+    blocks = spread_blocks(new_part, cohorts, 2).reshape(cohorts, hidden, owner_width)
+    new_weights = blocks.transpose(1, 0, 2).reshape(hidden, depth)
+    return (new_weights, new_momentum)
+
+
+def sum_body(client_tokens, targets, weights, momentum, noise_now, noise_prev):
     depth = weights.shape[1]
     clients = client_tokens.shape[1]
     round_block = lax.all_gather(client_tokens[0], "fsdp", axis=2, tiled=True)
     errors, squared, rate = client_errors(round_block, targets[0], weights)
     squared = lax.psum(squared, "fsdp")
-    cohort_sum = weighted_sum(errors, -rate * clip_factor(squared), round_block)
+    cohort_sum = weighted_sum(
+        errors, (-rate * clip_factor(squared))[:, None, None], round_block
+    )
     totals = lax.psum_scatter(cohort_sum, "cohort", scatter_dimension=1, tiled=True)
     owner_width = totals.shape[1]
     owner_start = lax.axis_index("cohort") * owner_width
@@ -103,6 +482,14 @@
     return (new_weights, new_momentum)
 
 
+def body(client_tokens, *others):
+    _, clients, steps, count, _ = client_tokens.shape
+    hidden = others[1].shape[0]
+    rank = clients * steps * count * lax.axis_size("fsdp")
+    few = rank <= hidden and lax.axis_size("cohort") % 2 == 0 and lax.axis_size("fsdp") % 2 == 0
+    return (factor_body if few else sum_body)(client_tokens, *others)
+
+
 def solution(mesh):
     in_specs = (
         P("cohort", None, None, "fsdp", None),

time: 289 us -> 170 us (0.59)
  waiting for transfers between devices: 214 us -> 0 us
  Pallas kernels: 0 us -> 130 us
  blocking collectives: 19.2 us -> 0 us
  between operations: 13.8 us -> 0.8 us
  other arithmetic: 7.99 us -> 1.59 us
    pallas_call x0 -> x3, Pallas kernels: none -> 130 us  [the longest x1 56.4 us: gather_tokens(): pl.pallas_call(lambda *refs: gather_kernel(cohorts, shards, *refs), name=...]
    all_gather x2 -> x0, waiting for transfers between devices: 117 us -> none  [the longest x1 69.9 us: body(): round_block = lax.all_gather(client_tokens[0], 'fsdp', axis=2, tiled=True)]
    reduce_scatter x1 -> x0, waiting for transfers between devices: 96.1 us -> none  [body(): lax.psum_scatter(cohort_sum, 'cohort', scatter_dimension=1, tiled=True)]
    psum x1 -> x0, blocking collectives: 19.2 us -> none  [body(): squared = lax.psum(squared, 'fsdp')]
    convert_element_type x2 -> x0, other arithmetic: 7.26 us -> none  [the longest x1 6.87 us: body(): new_part = (base_part + SERVER_LR * new_momentum).astype(jnp.bfloat16)]
    reshape x0 -> x2, local copies, waits for them, and re-layouts: none -> 7.15 us  [the longest x1 6.14 us: factor_body(): new_weights = blocks.transpose(1, 0, 2).reshape(hidden, depth)]
    unnamed x8 -> x13, local copies, waits for them, and re-layouts: 7.25 us -> 1.28 us
    dot_general x1, matrix products: 4.39 us -> 1.1 us  [client_errors(): jnp.einsum('ksd,ktd->kst', flat, flat, preferred_element_type=jnp.float32)]
  transfers between devices with their start and end apart: 3 -> 0, of which waited for: 3 -> 0; matrix products, arithmetic and copies ran while one was open for 0% -> 0% of each run, Pallas kernels for 0% -> 0%
where the time goes in v2:
time: 170 us
  Pallas kernels  130 us (76%)
  matrix products  27.8 us (16%)
  local copies, waits for them, and re-layouts  9.57 us (6%)
    pallas_call x1, Pallas kernels, gather_tokens(): pl.pallas_call(lambda *refs: gather_kernel(cohorts, shards, *refs), name=...  56.4 us
    pallas_call x1, Pallas kernels, spread_blocks(): pl.pallas_call(lambda *refs: blocks_kernel(cohorts, *refs), name='spread_...  41 us
    pallas_call x1, Pallas kernels, spread_errors(): pl.pallas_call(lambda *refs: errors_kernel(cohorts, shards, *refs), name=...  32.4 us
    dot_general x2, matrix products, weighted_sum(): lax.dot_general(part.reshape(-1, hidden), tokens, dims, preferred_element...  15.8 us
    dot_general x1, matrix products, client_errors(): lax.dot_general(flat.reshape(clients * steps * count, depth), weights, ((...  9.16 us
    reshape x1, local copies, waits for them, and re-layouts, factor_body(): new_weights = blocks.transpose(1, 0, 2).reshape(hidden, depth)  6.14 us

profile of v2, /device:TPU:0, one launch (start us, length us, event | category | flops | bytes accessed | tf_op | source)
XLA Modules:
  0.0 169.6 jit_solution(15950668999237918245)
XLA Ops:
  0.6 1.3 copy.30
  1.9 56.4 %gather_tokens.1 = (bf16[8,64,3584]{2,1,0:T(8,128)(2,1)}, bf16[4,8,64,896]{3,2,1,0:T(8,128)(2,1)}) custom-call(bf16[64,3584]{1,0:T(8,128)(2,1)} %bitcast.103), custom_call_target="tpu_custom_call" | custom-call | tf_op jit(solution)/shard_map/gather_tokens/pallas_call | solution.py:204
  58.3 0.0 copy-start
  58.3 9.2 %fusion.1 = f32[4,2,64,896]{3,2,1,0:T(8,128)S(1)} fusion(bf16[896,3584]{1,0:T(8,128)(2,1)} %param.8, bf16[4,2,8,8,3584]{4,3,1,0,2:T(8,128)(2,1)} %bitcast.96), kind=kOutput, calls=%fused_computation.3 | convolution fusion | flops 3288334336 | bytes 11927552 | tf_op jit(solution)/shard_map/dot_general | solution.py:384
  67.5 0.0 copy-done
  67.5 0.3 copy.14
  67.9 1.1 fusion.28
  69.0 0.7 fusion.21
  69.7 1.2 fusion.19
  70.9 0.5 fusion.13
  71.4 0.1 pad_maximum_fusion
  71.5 0.0 copy-start.5
  71.5 1.0 copy.18
  72.6 0.6 broadcast_in_dim.2.refs_1_
  73.2 32.4 %spread_errors.1 = (bf16[4,8,64,896]{3,2,1,0:T(8,128)(2,1)}, f32[4,4,128]{2,1,0:T(4,128)}) custom-call(bf16[8,64,896]{2,1,0:T(8,128)(2,1)} %bitcast.98, f32[4,128]{1,0:T(4,128)} %broadcast_in_dim.2.refs_1_), custom_call_target="tpu_custom_call" | custom-call | tf_op jit(solution)/shard_map/spread_errors/pallas_call | solution.py:352
  105.6 0.8 multiply_reduce_fusion
  106.4 0.1 mul.230
  106.5 0.1 mul.231
  106.6 0.0 copy-start.4
  106.6 7.4 %fusion.3 = f32[896,896,1,1]{1,0,3,2:T(8,128)S(1)} fusion(bf16[4,8,64,896]{3,2,1,0:T(8,128)(2,1)} %get-tuple-element.9, bf16[4,8,64,896]{3,2,1,0:T(8,128)(2,1)} %get-tuple-element.7, f32[4,64]{1,0:T(4,128)S(1)} %mul.231), kind=kOutput, calls=%fused_computation.5 | convolution fusion | flops 3293839360 | bytes 10552320 | tf_op jit(solution)/shard_map/dot_general | solution.py:415
  114.1 0.0 copy-done.5
  114.1 8.4 %add_convert_fusion = (bf16[896,896]{1,0:T(8,128)(2,1)}, f32[896,896]{1,0:T(8,128)}) fusion(bf16[896,3584]{1,0:T(8,128)(2,1)} %param.8, s32[]{:T(128)S(6)} %select_n.3, bf16[896,896]{1,0:T(8,128)(2,1)S(1)} %copy-done.4, bf16[896,896]{1,0:T(8,128)(2,1)S(1)} %copy-done.5, bf16[4,8,64,896]{3,2,1,0:T(8,128)(2,1)S(1)} %copy-done.1, ...), kind=kOutput, calls=%fused_computation.14 | convolution fusion | flops 3310583808 | bytes 23397380 | tf_op jit(solution)/shard_map/dot_general | solution.py:415
  122.5 41.0 %spread_blocks.1 = bf16[4,8,112,896]{3,2,1,0:T(8,128)(2,1)} custom-call(bf16[8,112,896]{2,1,0:T(8,128)(2,1)} %bitcast.102), custom_call_target="tpu_custom_call" | custom-call | tf_op jit(solution)/shard_map/spread_blocks/pallas_call | solution.py:289
  163.5 6.1 %copy.24 = bf16[4,112,8,896]{3,2,0,1:T(8,128)(2,1)} copy(bf16[4,112,8,896]{3,2,1,0:T(8,128)(2,1)} %bitcast.94) | data formatting | bytes 12845056 | tf_op jit(solution)/shard_map/reshape | solution.py:452
  (8 shorter events, 0.0 us)
Async XLA Ops:
  58.3 9.2 %copy-start = (bf16[8,64,3584]{2,1,0:T(8,128)(2,1)S(1)}, bf16[8,64,3584]{2,1,0:T(8,128)(2,1)}, u32[]{:S(2)}) copy-start(bf16[8,64,3584]{2,1,0:T(8,128)(2,1)} %get-tuple-element.6) | copy-start | bytes 11010052
  71.5 42.6 %copy-start.5 = (bf16[896,896]{1,0:T(8,128)(2,1)S(1)}, bf16[896,896]{1,0:T(8,128)(2,1)}, u32[]{:S(2)}) copy-start(bf16[896,896]{1,0:T(8,128)(2,1)} %param.10) | copy-start | bytes 4816900
  106.6 7.5 %copy-start.1 = (bf16[4,8,64,896]{3,2,1,0:T(8,128)(2,1)S(1)}, bf16[4,8,64,896]{3,2,1,0:T(8,128)(2,1)}, u32[]{:S(2)}) copy-start(bf16[4,8,64,896]{3,2,1,0:T(8,128)(2,1)} %get-tuple-element.9) | copy-start | bytes 11010052
  106.6 7.5 %copy-start.2 = (bf16[4,8,64,896]{3,2,1,0:T(8,128)(2,1)S(1)}, bf16[4,8,64,896]{3,2,1,0:T(8,128)(2,1)}, u32[]{:S(2)}) copy-start(bf16[4,8,64,896]{3,2,1,0:T(8,128)(2,1)} %get-tuple-element.7) | copy-start | bytes 11010052
  106.6 7.5 %copy-start.3 = (f32[896,896]{1,0:T(8,128)S(1)}, f32[896,896]{1,0:T(8,128)}, u32[]{:S(2)}) copy-start(f32[896,896]{1,0:T(8,128)} %param.9) | copy-start | bytes 9633796
  106.6 7.5 %copy-start.4 = (bf16[896,896]{1,0:T(8,128)(2,1)S(1)}, bf16[896,896]{1,0:T(8,128)(2,1)}, u32[]{:S(2)}) copy-start(bf16[896,896]{1,0:T(8,128)(2,1)} %param.11) | copy-start | bytes 4816900

commit v3 on v2

--- a/solution.py
+++ b/solution.py
@@ -78,147 +78,158 @@
         signal(other, f)
     pl.semaphore_wait(pltpu.get_barrier_semaphore(), cohorts + 2)
 
-    def up(slot, source):
-        return remote(source, all_ref.at[slot], to_up.at[slot], got.at[slot], c, f + 2)
-
-    def down(slot, source):
-        return remote(source, all_ref.at[slot], to_down.at[slot], got.at[slot], c, f - 2)
-
-    def across(slot, source):
-        return remote(source, all_ref.at[slot], to_pair.at[slot], got.at[slot], c, pair)
+    pieces = own_ref.shape[0]
+
+    def up(slot, piece, source):
+        return remote(
+            source, all_ref.at[slot, piece], to_up.at[slot, piece], got.at[slot, piece], c, f + 2
+        )
+
+    def down(slot, piece, source):
+        return remote(
+            source, all_ref.at[slot, piece], to_down.at[slot, piece], got.at[slot, piece], c, f - 2
+        )
+
+    def across(slot, piece, source):
+        return remote(
+            source, all_ref.at[slot, piece], to_pair.at[slot, piece], got.at[slot, piece], c, pair
+        )
 
     def columns(source, owner):
         return source.at[:, pl.ds(pl.multiple_of(owner * width, 128), width)]
 
-    def cuts(slot, source):
+    def cuts(slot, piece, source):
         copies = [
             remote(
                 columns(source, other),
-                cut_ref.at[c, slot],
-                to_cut.at[at, slot],
-                got_cut.at[c, slot],
+                cut_ref.at[c, slot, piece],
+                to_cut.at[at, slot, piece],
+                got_cut.at[c, slot, piece],
                 other,
                 f,
             )
             for at, other in enumerate(others)
         ]
-        own = pltpu.make_async_copy(columns(source, c), cut_ref.at[c, slot], kept_cut.at[slot])
+        own = pltpu.make_async_copy(
+            columns(source, c), cut_ref.at[c, slot, piece], kept_cut.at[slot, piece]
+        )
         return copies + [own]
 
-    def arrived(slot):
-        remote(
-            all_ref.at[slot], all_ref.at[slot], to_pair.at[slot], got.at[slot], c, pair
-        ).wait_recv()
+    def arrived(slot, piece):
+        across(slot, piece, own_ref.at[0]).wait_recv()
 
     def start(copies):
         for copy in copies:
             copy.start()
 
     keep = pltpu.make_async_copy(own_ref, all_ref.at[f], kept)
-
-    @pl.when(row + 1 < rows)
-    def _():
-        up(f, own_ref).start()
-
-    @pl.when(row > 0)
-    def _():
-        down(f, own_ref).start()
-
-    across(f, own_ref).start()
-    start(cuts(f, own_ref))
+    for piece in range(pieces):
+
+        @pl.when(row + 1 < rows)
+        def _():
+            up(f, piece, own_ref.at[piece]).start()
+
+        @pl.when(row > 0)
+        def _():
+            down(f, piece, own_ref.at[piece]).start()
+
+        across(f, piece, own_ref.at[piece]).start()
+        start(cuts(f, piece, own_ref.at[piece]))
     keep.start()
 
     for step in range(1, rows + 1):
-
-        @pl.when(row >= step)
-        def _():
-            slot = f - 2 * step
-            arrived(slot)
-
-            @pl.when(row + 1 < rows)
+        last = step - 1
+        for piece in range(pieces):
+
+            @pl.when(row >= step)
             def _():
-                up(slot, all_ref.at[slot]).start()
-
-            across(slot, all_ref.at[slot]).start()
-            start(cuts(slot, all_ref.at[slot]))
-
-        @pl.when(row + step < rows)
-        def _():
-            slot = f + 2 * step
-            arrived(slot)
-
-            @pl.when(row > 0)
+                slot = f - 2 * step
+                arrived(slot, piece)
+
+                @pl.when(row + 1 < rows)
+                def _():
+                    up(slot, piece, all_ref.at[slot, piece]).start()
+
+                across(slot, piece, all_ref.at[slot, piece]).start()
+                start(cuts(slot, piece, all_ref.at[slot, piece]))
+
+            @pl.when(row + step < rows)
             def _():
-                down(slot, all_ref.at[slot]).start()
-
-            across(slot, all_ref.at[slot]).start()
-            start(cuts(slot, all_ref.at[slot]))
-
-        last = step - 1
-
-        @pl.when(row >= last)
-        def _():
-            slot = pair - 2 * last
-            arrived(slot)
-            start(cuts(slot, all_ref.at[slot]))
-
-        if last > 0:
-
-            @pl.when(row + last < rows)
+                slot = f + 2 * step
+                arrived(slot, piece)
+
+                @pl.when(row > 0)
+                def _():
+                    down(slot, piece, all_ref.at[slot, piece]).start()
+
+                across(slot, piece, all_ref.at[slot, piece]).start()
+                start(cuts(slot, piece, all_ref.at[slot, piece]))
+
+            @pl.when(row >= last)
             def _():
-                slot = pair + 2 * last
-                arrived(slot)
-                start(cuts(slot, all_ref.at[slot]))
+                slot = pair - 2 * last
+                arrived(slot, piece)
+                start(cuts(slot, piece, all_ref.at[slot, piece]))
+
+            if last > 0:
+
+                @pl.when(row + last < rows)
+                def _():
+                    slot = pair + 2 * last
+                    arrived(slot, piece)
+                    start(cuts(slot, piece, all_ref.at[slot, piece]))
 
     keep.wait()
-    for line in range(rows):
-        slot = 2 * line + side
-
-        @pl.when((row + 1 < rows) & (line <= row))
-        def _():
-            up(slot, own_ref).wait_send()
-
-        @pl.when((row > 0) & (line >= row))
-        def _():
-            down(slot, own_ref).wait_send()
-
-        across(slot, own_ref).wait_send()
-    for slot in range(shards):
-        *sent, own = cuts(slot, own_ref)
-        own.wait()
-        for copy in sent:
-            copy.wait_send()
-        for other in others:
-            remote(
-                cut_ref.at[other, slot],
-                cut_ref.at[other, slot],
-                to_pair.at[slot],
-                got_cut.at[other, slot],
-                other,
-                f,
-            ).wait_recv()
+    for piece in range(pieces):
+        source = own_ref.at[piece]
+        for line in range(rows):
+            slot = 2 * line + side
+
+            @pl.when((row + 1 < rows) & (line <= row))
+            def _():
+                up(slot, piece, source).wait_send()
+
+            @pl.when((row > 0) & (line >= row))
+            def _():
+                down(slot, piece, source).wait_send()
+
+            across(slot, piece, source).wait_send()
+        for slot in range(shards):
+            *sent, own = cuts(slot, piece, source)
+            own.wait()
+            for copy in sent:
+                copy.wait_send()
+            for other in others:
+                remote(
+                    columns(source, c),
+                    cut_ref.at[other, slot, piece],
+                    to_pair.at[slot, piece],
+                    got_cut.at[other, slot, piece],
+                    other,
+                    f,
+                ).wait_recv()
 
 
 def gather_tokens(tokens, cohorts, shards):
-    count, depth = tokens.shape
+    pieces, count, depth = tokens.shape
     return pl.pallas_call(
         lambda *refs: gather_kernel(cohorts, shards, *refs),
         name="gather_tokens",
         out_shape=(
-            jax.ShapeDtypeStruct((shards, count, depth), tokens.dtype),
-            jax.ShapeDtypeStruct((cohorts, shards, count, depth // cohorts), tokens.dtype),
+            jax.ShapeDtypeStruct((shards, pieces, count, depth), tokens.dtype),
+            jax.ShapeDtypeStruct((cohorts, shards, pieces, count, depth // cohorts), tokens.dtype),
         ),
         in_specs=[IN_VMEM],
         out_specs=(IN_VMEM, ANY),
         scratch_shapes=[
-            DMA((shards,)),
-            DMA((cohorts, shards)),
-            DMA((shards,)),
-            DMA((shards,)),
-            DMA((shards,)),
-            DMA((cohorts - 1, shards)),
+            DMA((shards, pieces)),
+            DMA((cohorts, shards, pieces)),
+            DMA((shards, pieces)),
+            DMA((shards, pieces)),
+            DMA((shards, pieces)),
+            DMA((cohorts - 1, shards, pieces)),
             DMA,
-            DMA((shards,)),
+            DMA((shards, pieces)),
         ],
         compiler_params=pltpu.CompilerParams(
             collective_id=0, has_side_effects=True, vmem_limit_bytes=60 << 20
@@ -226,7 +237,7 @@
     )(tokens)
 
 
-def spread_kernel(cohorts, own_ref, all_ref, got, to_far, to_pair, kept):
+def spread_kernel(cohorts, own_ref, all_ref, got, to_far, to_pair, kept, meanwhile=None):
     c, f = lax.axis_index("cohort"), lax.axis_index("fsdp")
     pair = c + 1 - 2 * (c % 2)
     pieces = own_ref.shape[0]
@@ -254,6 +265,8 @@
             outward(at, piece).start()
     for piece in range(pieces):
         across(c, piece, own_ref.at[piece]).start()
+    if meanwhile is not None:
+        meanwhile()
     for piece in range(pieces):
         for slot in far:
             copy = across(slot, piece, all_ref.at[slot, piece])
@@ -326,19 +339,21 @@
             total, norm_ref.at[source], to_norm.at[at], got_norm.at[source], cohort_others[at], f
         )
 
+    def sum_norms():
+        parts[pl.ds(f, 1)] = part_ref[...][None]
+        for at, other in enumerate(others):
+            part(at, other).wait_recv()
+        summed = parts[0]
+        for at in range(1, shards):
+            summed = summed + parts[at]
+        total[...] = summed
+        norm_ref[pl.ds(c, 1)] = summed[None]
+        for at in range(len(cohort_others)):
+            norm(at, c).start()
+
     for at in range(len(others)):
         part(at, f).start()
-    parts[pl.ds(f, 1)] = part_ref[...][None]
-    for at, other in enumerate(others):
-        part(at, other).wait_recv()
-    summed = parts[0]
-    for at in range(1, shards):
-        summed = summed + parts[at]
-    total[...] = summed
-    norm_ref[pl.ds(c, 1)] = summed[None]
-    for at in range(len(cohort_others)):
-        norm(at, c).start()
-    spread_kernel(cohorts, own_ref, all_ref, got, to_far, to_pair, kept)
+    spread_kernel(cohorts, own_ref, all_ref, got, to_far, to_pair, kept, sum_norms)
     for at, other in enumerate(cohort_others):
         norm(at, other).wait_recv()
         norm(at, c).wait_send()
@@ -376,17 +391,11 @@
     )(errors, tile)
 
 
-def client_errors(tokens, targets, weights):
+def client_errors(tokens, products, targets):
     clients, steps, count, depth = tokens.shape
     rate = LOCAL_LR / (count * math.sqrt(depth))
     scale = 1.0 / math.sqrt(depth)
     flat = tokens.reshape(clients, steps * count, depth)
-    products = lax.dot_general(
-        flat.reshape(clients * steps * count, depth),
-        weights,
-        (((1,), (1,)), ((), ())),
-        preferred_element_type=jnp.float32,
-    ).reshape(clients, steps, count, weights.shape[0])
     gram = jnp.einsum("ksd,ktd->kst", flat, flat, preferred_element_type=jnp.float32)
     errors = []
     for step in range(steps):
@@ -419,14 +428,26 @@
     )
 
 
+def products_of(tokens, weights):
+    return lax.dot_general(
+        tokens, weights, (((1,), (1,)), ((), ())), preferred_element_type=jnp.float32
+    )
+
+
 def factor_body(client_tokens, targets, weights, momentum, noise_now, noise_prev):
     cohorts, shards = lax.axis_size("cohort"), lax.axis_size("fsdp")
     hidden, depth = weights.shape
     _, clients, steps, count, _ = client_tokens.shape
-    gathered, columns = gather_tokens(client_tokens.reshape(-1, depth), cohorts, shards)
+    pieces = max(clients * steps * count // 16, 1)
+    gathered, columns = gather_tokens(
+        client_tokens.reshape(pieces, -1, depth), cohorts, shards
+    )
+    products = products_of(gathered.reshape(-1, depth), weights)
+    products = products.reshape(shards, clients, steps, count, hidden)
+    products = products.transpose(1, 2, 0, 3, 4).reshape(clients, steps, shards * count, hidden)
     tokens = gathered.reshape(shards, clients, steps, count, depth)
     tokens = tokens.transpose(1, 2, 0, 3, 4).reshape(clients, steps, shards * count, depth)
-    errors, squared, rate = client_errors(tokens, targets[0], weights)
+    errors, squared, rate = client_errors(tokens, products, targets[0])
     errors = errors.reshape(clients, steps, shards, count, hidden).transpose(2, 0, 1, 3, 4)
     errors, squared = spread_errors(errors.reshape(shards, -1, hidden), squared, cohorts, shards)
     factors = -rate * clip_factor(squared[:, :, 0])
@@ -457,7 +478,9 @@
     depth = weights.shape[1]
     clients = client_tokens.shape[1]
     round_block = lax.all_gather(client_tokens[0], "fsdp", axis=2, tiled=True)
-    errors, squared, rate = client_errors(round_block, targets[0], weights)
+    products = products_of(round_block.reshape(-1, depth), weights)
+    products = products.reshape(round_block.shape[:3] + weights.shape[:1])
+    errors, squared, rate = client_errors(round_block, products, targets[0])
     squared = lax.psum(squared, "fsdp")
     cohort_sum = weighted_sum(
         errors, (-rate * clip_factor(squared))[:, None, None], round_block

time: 170 us -> 164 us (0.965)
  Pallas kernels: 130 us -> 124 us
    pallas_call x1, Pallas kernels: 32.4 us -> 27.1 us  [spread_errors(): pl.pallas_call(lambda *refs: errors_kernel(cohorts, shards, *refs), name=...]
where the time goes in v3:
time: 164 us
  Pallas kernels  124 us (76%)
  matrix products  26.6 us (16%)
  local copies, waits for them, and re-layouts  10.7 us (7%)
    pallas_call x1, Pallas kernels, gather_tokens(): pl.pallas_call(lambda *refs: gather_kernel(cohorts, shards, *refs), name=...  56.1 us
    pallas_call x1, Pallas kernels, spread_blocks(): pl.pallas_call(lambda *refs: blocks_kernel(cohorts, *refs), name='spread_...  41 us
    pallas_call x1, Pallas kernels, spread_errors(): pl.pallas_call(lambda *refs: errors_kernel(cohorts, shards, *refs), name=...  27.1 us
    dot_general x2, matrix products, weighted_sum(): lax.dot_general(part.reshape(-1, hidden), tokens, dims, preferred_element...  14.7 us
    dot_general x1, matrix products, products_of(): lax.dot_general(tokens, weights, (((1,), (1,)), ((), ())), preferred_elem...  9.09 us
    reshape x1, local copies, waits for them, and re-layouts, factor_body(): new_weights = blocks.transpose(1, 0, 2).reshape(hidden, depth)  6.14 us

profile of v3, /device:TPU:0, one launch (start us, length us, event | category | flops | bytes accessed | tf_op | source)
XLA Modules:
  0.0 163.9 jit_solution(10904062552098199127)
XLA Ops:
  0.6 1.3 copy.28
  1.9 56.1 %gather_tokens.1 = (bf16[8,4,16,3584]{3,2,1,0:T(8,128)(2,1)}, bf16[4,8,4,16,896]{4,3,2,1,0:T(8,128)(2,1)}) custom-call(bf16[4,16,3584]{2,1,0:T(8,128)(2,1)} %bitcast.116), custom_call_target="tpu_custom_call" | custom-call | tf_op jit(solution)/shard_map/gather_tokens/pallas_call | solution.py:215
  58.0 9.1 %fusion.17 = f32[4,2,8,8,896]{4,3,1,0,2:T(8,128)S(1)} fusion(bf16[896,3584]{1,0:T(8,128)(2,1)} %param.8, bf16[8,4,16,3584]{3,2,1,0:T(8,128)(2,1)} %get-tuple-element.6), kind=kOutput, calls=%fused_computation.16 | convolution fusion | flops 3288334336 | bytes 11927552 | tf_op jit(solution)/shard_map/dot_general | solution.py:432
  67.1 0.0 copy-start
  67.1 0.1 copy.27
  67.2 0.7 fusion.31
  67.9 1.2 copy-done
  69.1 0.3 copy.16
  69.5 1.1 fusion.37
  70.6 1.2 fusion.29
  71.8 0.0 copy-start.1
  71.8 0.5 fusion.23
  72.3 0.1 pad_maximum_fusion
  72.4 1.0 copy.17
  73.4 0.6 broadcast_in_dim.2.refs_1_
  74.1 27.1 %spread_errors.1 = (bf16[4,8,64,896]{3,2,1,0:T(8,128)(2,1)}, f32[4,4,128]{2,1,0:T(4,128)}) custom-call(bf16[8,64,896]{2,1,0:T(8,128)(2,1)} %bitcast.111, f32[4,128]{1,0:T(4,128)} %broadcast_in_dim.2.refs_1_), custom_call_target="tpu_custom_call" | custom-call | tf_op jit(solution)/shard_map/spread_errors/pallas_call | solution.py:367
  101.2 0.8 multiply_reduce_fusion
  102.0 0.0 copy-start.3
  102.1 0.0 copy-start.4
  102.1 0.0 copy-start.5
  102.1 6.4 %fusion.5 = f32[896,896,1,1,1]{1,0,4,3,2:T(8,128)S(1)} fusion(bf16[4,8,4,16,896]{4,3,2,1,0:T(8,128)(2,1)S(1)} %copy-done.1, bf16[4,8,4,16,896]{4,3,2,1,0:T(8,128)(2,1)} %bitcast.117, f32[4,4]{1,0:T(4,128)S(1)} %multiply_reduce_fusion), kind=kOutput, calls=%fused_computation.6 | convolution fusion | flops 3299344384 | bytes 10551360 | tf_op jit(solution)/shard_map/dot_general | solution.py:424
  108.5 8.3 %add_convert_fusion = (bf16[896,896]{1,0:T(8,128)(2,1)}, f32[896,896]{1,0:T(8,128)}) fusion(bf16[896,3584]{1,0:T(8,128)(2,1)} %param.8, s32[]{:T(128)S(6)} %select_n.3, bf16[896,896]{1,0:T(8,128)(2,1)S(1)} %copy-done.4, bf16[896,896]{1,0:T(8,128)(2,1)S(1)} %copy-done.5, f32[896,896,1,1,1]{1,0,4,3,2:T(8,128)S(1)} %fusion.5, ...), kind=kOutput, calls=%fused_computation.14 | convolution fusion | flops 3305078784 | bytes 23396420 | tf_op jit(solution)/shard_map/dot_general | solution.py:424
  116.8 41.0 %spread_blocks.1 = bf16[4,8,112,896]{3,2,1,0:T(8,128)(2,1)} custom-call(bf16[8,112,896]{2,1,0:T(8,128)(2,1)} %bitcast.115), custom_call_target="tpu_custom_call" | custom-call | tf_op jit(solution)/shard_map/spread_blocks/pallas_call | solution.py:302
  157.8 6.1 %copy.24 = bf16[4,112,8,896]{3,2,0,1:T(8,128)(2,1)} copy(bf16[4,112,8,896]{3,2,1,0:T(8,128)(2,1)} %bitcast.106) | data formatting | bytes 12845056 | tf_op jit(solution)/shard_map/reshape | solution.py:473
  (7 shorter events, 0.0 us)
Async XLA Ops:
  67.1 2.0 %copy-start = (bf16[8,4,16,3584]{3,2,1,0:T(8,128)(2,1)S(1)}, bf16[8,4,16,3584]{3,2,1,0:T(8,128)(2,1)}, u32[]{:S(2)}) copy-start(bf16[8,4,16,3584]{3,2,1,0:T(8,128)(2,1)} %get-tuple-element.6) | copy-start | bytes 11010052
  71.8 30.2 %copy-start.1 = (bf16[4,8,4,16,896]{4,3,2,1,0:T(8,128)(2,1)S(1)}, bf16[4,8,4,16,896]{4,3,2,1,0:T(8,128)(2,1)}, u32[]{:S(2)}) copy-start(bf16[4,8,4,16,896]{4,3,2,1,0:T(8,128)(2,1)} %get-tuple-element.9) | copy-start | bytes 11010052
  102.0 6.4 %copy-start.2 = (bf16[4,8,64,896]{3,2,1,0:T(8,128)(2,1)S(1)}, bf16[4,8,64,896]{3,2,1,0:T(8,128)(2,1)}, u32[]{:S(2)}) copy-start(bf16[4,8,64,896]{3,2,1,0:T(8,128)(2,1)} %get-tuple-element.7) | copy-start | bytes 11010052
  102.0 6.4 %copy-start.3 = (f32[896,896]{1,0:T(8,128)S(1)}, f32[896,896]{1,0:T(8,128)}, u32[]{:S(2)}) copy-start(f32[896,896]{1,0:T(8,128)} %param.9) | copy-start | bytes 9633796
  102.1 6.4 %copy-start.4 = (bf16[896,896]{1,0:T(8,128)(2,1)S(1)}, bf16[896,896]{1,0:T(8,128)(2,1)}, u32[]{:S(2)}) copy-start(bf16[896,896]{1,0:T(8,128)(2,1)} %param.11) | copy-start | bytes 4816900
  102.1 6.4 %copy-start.5 = (bf16[896,896]{1,0:T(8,128)(2,1)S(1)}, bf16[896,896]{1,0:T(8,128)(2,1)}, u32[]{:S(2)}) copy-start(bf16[896,896]{1,0:T(8,128)(2,1)} %param.10) | copy-start | bytes 4816900

commit v4 on v3

--- a/solution.py
+++ b/solution.py
@@ -237,13 +237,14 @@
     )(tokens)
 
 
-def spread_kernel(cohorts, own_ref, all_ref, got, to_far, to_pair, kept, meanwhile=None):
+def spread_kernel(cohorts, own_ref, all_ref, got, to_far, to_pair, kept, meanwhile=None, produce=None):
     c, f = lax.axis_index("cohort"), lax.axis_index("fsdp")
     pair = c + 1 - 2 * (c % 2)
     pieces = own_ref.shape[0]
     far = [(c + 2 * j) % cohorts for j in range(1, cohorts // 2)]
     keep = pltpu.make_async_copy(own_ref, all_ref.at[c], kept)
-    keep.start()
+    if produce is None:
+        keep.start()
 
     def outward(at, piece):
         return remote(
@@ -260,11 +261,19 @@
             source, all_ref.at[slot, piece], to_pair.at[slot, piece], got.at[slot, piece], pair, f
         )
 
-    for piece in range(pieces):
+    def send(piece):
+        if produce is not None:
+            produce(piece)
         for at in range(len(far)):
             outward(at, piece).start()
-    for piece in range(pieces):
         across(c, piece, own_ref.at[piece]).start()
+
+    if produce is None:
+        for piece in range(pieces):
+            send(piece)
+    else:
+        pl.loop(0, pieces)(send)
+        keep.start()
     if meanwhile is not None:
         meanwhile()
     for piece in range(pieces):
@@ -292,29 +301,60 @@
     pl.semaphore_wait(pltpu.get_barrier_semaphore(), cohorts // 2 + len(others))
 
 
-def blocks_kernel(cohorts, own_ref, all_ref, got, to_far, to_pair, kept):
+def server_kernel(
+    cohorts, gain, high, low, tokens, base, momentum, now, prev,
+    all_ref, momentum_ref, fresh, got, to_far, to_pair, kept,
+):
+    lines = fresh.shape[1]
+
+    def produce(piece):
+        here = pl.ds(pl.multiple_of(piece * lines, lines), lines)
+        both = lax.dot_general(
+            jnp.concatenate([high[:, here], low[:, here]], axis=1),
+            tokens[...],
+            (((0,), (0,)), ((), ())),
+            preferred_element_type=jnp.float32,
+        )
+        noise = (
+            NOISE_STD
+            * CLIP_BOUND
+            * (now[here].astype(jnp.float32) - BAND_COEF * prev[here].astype(jnp.float32))
+        )
+        aggregate = gain * (both[:lines] + both[lines:] + noise)
+        new_momentum = MOMENTUM_DECAY * momentum[here] + aggregate
+        momentum_ref[here, :] = new_momentum
+        fresh[pl.ds(piece, 1)] = (
+            (base[here].astype(jnp.float32) + SERVER_LR * new_momentum).astype(fresh.dtype)[None]
+        )
+
     greet(cohorts, lax.axis_index("cohort"), lax.axis_index("fsdp"), [])
-    spread_kernel(cohorts, own_ref, all_ref, got, to_far, to_pair, kept)
-
-
-def spread_blocks(block, cohorts, collective_id):
-    pieces = block.shape[0]
+    spread_kernel(cohorts, fresh, all_ref, got, to_far, to_pair, kept, produce=produce)
+
+
+def serve(high, low, tokens, base, momentum, now, prev, gain, cohorts):
+    hidden, width = base.shape
+    lines = math.gcd(hidden, 128)
+    pieces = hidden // lines
     return pl.pallas_call(
-        lambda *refs: blocks_kernel(cohorts, *refs),
-        name="spread_blocks",
-        out_shape=jax.ShapeDtypeStruct((cohorts,) + block.shape, block.dtype),
-        in_specs=[IN_VMEM],
-        out_specs=ANY,
+        lambda *refs: server_kernel(cohorts, gain, *refs),
+        name="serve",
+        out_shape=(
+            jax.ShapeDtypeStruct((cohorts, pieces, lines, width), base.dtype),
+            jax.ShapeDtypeStruct(momentum.shape, momentum.dtype),
+        ),
+        in_specs=[IN_VMEM] * 7,
+        out_specs=(ANY, IN_VMEM),
         scratch_shapes=[
+            pltpu.VMEM((pieces, lines, width), base.dtype),
             DMA((cohorts, pieces)),
             DMA((max(cohorts // 2 - 1, 1), pieces)),
             DMA((cohorts, pieces)),
             DMA,
         ],
         compiler_params=pltpu.CompilerParams(
-            collective_id=collective_id, has_side_effects=True, vmem_limit_bytes=60 << 20
+            collective_id=2, has_side_effects=True, vmem_limit_bytes=60 << 20
         ),
-    )(block)
+    )(high, low, tokens, base, momentum, now, prev)
 
 
 def errors_kernel(
@@ -413,18 +453,20 @@
     return errors, squared, rate
 
 
-def weighted_sum(errors, factors, tokens):
-    hidden, width = errors.shape[-1], tokens.shape[-1]
+def split_scaled(errors, factors):
     scaled = errors.astype(jnp.float32) * factors
     high = scaled.astype(jnp.bfloat16)
     low = (scaled - high.astype(jnp.float32)).astype(jnp.bfloat16)
-    tokens = tokens.reshape(-1, width)
+    hidden = errors.shape[-1]
+    return high.reshape(-1, hidden), low.reshape(-1, hidden)
+
+
+def weighted_sum(errors, factors, tokens):
+    tokens = tokens.reshape(-1, tokens.shape[-1])
     dims = (((0,), (0,)), ((), ()))
     return sum(
-        lax.dot_general(
-            part.reshape(-1, hidden), tokens, dims, preferred_element_type=jnp.float32
-        )
-        for part in (high, low)
+        lax.dot_general(part, tokens, dims, preferred_element_type=jnp.float32)
+        for part in split_scaled(errors, factors)
     )
 
 
@@ -452,24 +494,23 @@
     errors, squared = spread_errors(errors.reshape(shards, -1, hidden), squared, cohorts, shards)
     factors = -rate * clip_factor(squared[:, :, 0])
     errors = errors.reshape(cohorts, shards, clients, steps * count, hidden)
-    totals = weighted_sum(errors, factors[:, None, :, None, None], columns)
-    owner_width = totals.shape[1]
+    high, low = split_scaled(errors, factors[:, None, :, None, None])
+    owner_width = columns.shape[-1]
     owner_start = lax.axis_index("cohort") * owner_width
-    base_part = lax.dynamic_slice_in_dim(weights, owner_start, owner_width, 1).astype(jnp.float32)
-    hidden_count = hidden * shards
-    noise = (
-        NOISE_STD
-        * CLIP_BOUND
-        * (noise_now.astype(jnp.float32) - BAND_COEF * noise_prev.astype(jnp.float32))
-    )
-    aggregate = (
-        math.sqrt(hidden_count * depth) / (cohorts * clients * CLIP_BOUND) * (totals + noise)
-    )
-    new_momentum = MOMENTUM_DECAY * momentum + aggregate
-    new_part = (base_part + SERVER_LR * new_momentum).astype(jnp.bfloat16)
-    pieces = math.gcd(hidden // 16, 8)
-    new_part = new_part.reshape(pieces, hidden // pieces, owner_width)
-    blocks = spread_blocks(new_part, cohorts, 2).reshape(cohorts, hidden, owner_width)
+    base_part = lax.dynamic_slice_in_dim(weights, owner_start, owner_width, 1)
+    gain = math.sqrt(hidden * shards * depth) / (cohorts * clients * CLIP_BOUND)
+    blocks, new_momentum = serve(
+        high,
+        low,
+        columns.reshape(-1, owner_width),
+        base_part,
+        momentum,
+        noise_now,
+        noise_prev,
+        gain,
+        cohorts,
+    )
+    blocks = blocks.reshape(cohorts, hidden, owner_width)
     new_weights = blocks.transpose(1, 0, 2).reshape(hidden, depth)
     return (new_weights, new_momentum)
 

time: 164 us -> 167 us (1.018)
  matrix products: 26.6 us -> 12 us
  Pallas kernels: 124 us -> 132 us
  other arithmetic: 1.59 us -> 6.7 us
  local copies, waits for them, and re-layouts: 10.7 us -> 15.4 us
    dot_general x2 -> x0, matrix products: 14.7 us -> none  [weighted_sum(): lax.dot_general(part.reshape(-1, hidden), tokens, dims, preferred_element...]
    pallas_call x1, Pallas kernels: 41 us -> 48.9 us  [serve(): pl.pallas_call(lambda *refs: server_kernel(cohorts, gain, *refs), name='s...]
    convert_element_type x0 -> x1, other arithmetic: none -> 5.11 us  [split_scaled(): low = (scaled - high.astype(jnp.float32)).astype(jnp.bfloat16)]
    dynamic_slice x0 -> x1, local copies, waits for them, and re-layouts: none -> 2.71 us  [factor_body(): base_part = lax.dynamic_slice_in_dim(weights, owner_start, owner_width, 1)]
    unnamed x13 -> x6, local copies, waits for them, and re-layouts: 2.46 us -> 4.12 us
where the time goes in v4:
time: 167 us
  Pallas kernels  132 us (79%)
  local copies, waits for them, and re-layouts  15.4 us (9%)
  matrix products  12 us (7%)
  other arithmetic  6.7 us (4%)
    pallas_call x1, Pallas kernels, gather_tokens(): pl.pallas_call(lambda *refs: gather_kernel(cohorts, shards, *refs), name=...  56 us
    pallas_call x1, Pallas kernels, serve(): pl.pallas_call(lambda *refs: server_kernel(cohorts, gain, *refs), name='s...  48.9 us
    pallas_call x1, Pallas kernels, spread_errors(): pl.pallas_call(lambda *refs: errors_kernel(cohorts, shards, *refs), name=...  27.1 us
    dot_general x1, matrix products, products_of(): lax.dot_general(tokens, weights, (((1,), (1,)), ((), ())), preferred_elem...  9.09 us
    reshape x1, local copies, waits for them, and re-layouts, factor_body(): new_weights = blocks.transpose(1, 0, 2).reshape(hidden, depth)  6.29 us
    convert_element_type x1, other arithmetic, split_scaled(): low = (scaled - high.astype(jnp.float32)).astype(jnp.bfloat16)  5.11 us
    unnamed x6, local copies, waits for them, and re-layouts  4.12 us

profile of v4, /device:TPU:0, one launch (start us, length us, event | category | flops | bytes accessed | tf_op | source)
XLA Modules:
  0.0 166.9 jit_solution(13272215576519609437)
XLA Ops:
  0.6 1.3 copy.26
  1.9 2.7 %constant_dynamic-slice_fusion.refs_3_ = bf16[896,896]{1,0:T(8,128)(2,1)} fusion(bf16[896,3584]{1,0:T(8,128)(2,1)} %param.8, s32[]{:T(128)S(6)} %select_n.3), kind=kLoop, calls=%fused_computation.41 | loop fusion | bytes 3211268 | tf_op jit(solution)/shard_map/dynamic_slice | solution.py:500
  4.6 56.0 %gather_tokens.1 = (bf16[8,4,16,3584]{3,2,1,0:T(8,128)(2,1)}, bf16[4,8,4,16,896]{4,3,2,1,0:T(8,128)(2,1)}) custom-call(bf16[4,16,3584]{2,1,0:T(8,128)(2,1)} %bitcast.104), custom_call_target="tpu_custom_call" | custom-call | tf_op jit(solution)/shard_map/gather_tokens/pallas_call | solution.py:215
  60.6 9.1 %fusion.6 = f32[4,2,8,8,896]{4,3,1,0,2:T(8,128)S(1)} fusion(bf16[896,3584]{1,0:T(8,128)(2,1)} %param.8, bf16[8,4,16,3584]{3,2,1,0:T(8,128)(2,1)} %get-tuple-element.8), kind=kOutput, calls=%fused_computation.8 | convolution fusion | flops 3288334336 | bytes 11927552 | tf_op jit(solution)/shard_map/dot_general | solution.py:474
  69.7 0.0 copy-start
  69.7 0.1 copy.25
  69.9 0.7 fusion.20
  70.6 1.2 copy-done
  71.8 0.3 copy.16
  72.1 1.1 fusion.26
  73.2 1.2 fusion.18
  74.4 0.5 fusion.12
  75.0 0.1 pad_maximum_fusion
  75.1 1.0 copy.17
  76.1 0.7 broadcast_in_dim.2.refs_1_
  76.7 27.1 %spread_errors.1 = (bf16[4,8,64,896]{3,2,1,0:T(8,128)(2,1)}, f32[4,4,128]{2,1,0:T(4,128)}) custom-call(bf16[8,64,896]{2,1,0:T(8,128)(2,1)} %bitcast.100, f32[4,128]{1,0:T(4,128)} %broadcast_in_dim.2.refs_1_), custom_call_target="tpu_custom_call" | custom-call | tf_op jit(solution)/shard_map/spread_errors/pallas_call | solution.py:407
  103.9 0.8 multiply_reduce_fusion
  104.7 0.1 mul.201
  104.8 0.1 mul.202
  104.9 5.1 %fusion.2 = (bf16[2048,896]{1,0:T(8,128)(2,1)}, bf16[2048,896]{1,0:T(8,128)(2,1)}) fusion(bf16[4,8,64,896]{3,2,1,0:T(8,128)(2,1)} %get-tuple-element.9, f32[2048]{0:T(1024)S(1)} %mul.202), kind=kLoop, calls=%fused_computation.3 | loop fusion | flops 11010048 | bytes 11018240 | tf_op jit(solution)/shard_map/convert_element_type | solution.py:459
  110.0 48.9 %serve.1 = (bf16[4,7,128,896]{3,2,1,0:T(8,128)(2,1)}, f32[896,896]{1,0:T(8,128)}) custom-call(bf16[2048,896]{1,0:T(8,128)(2,1)} %get-tuple-element.15.refs_0_, bf16[2048,896]{1,0:T(8,128)(2,1)} %get-tuple-element.14.refs_1_, bf16[2048,896]{1,0:T(8,128)(2,1)} %bitcast.98, bf16[896,896]{1,0:T(8,128)(2,1)} %constant_dynamic-slice_fusion.refs_3_, ...), custom_call_target="tpu_custom_call" | custom-call | tf_op jit(solution)/shard_map/serve/pallas_call | solution.py:338
  158.9 0.0 copy-start.1
  158.9 6.3 %copy.22 = bf16[4,112,8,896]{3,2,0,1:T(8,128)(2,1)} copy(bf16[4,112,8,896]{3,2,1,0:T(8,128)(2,1)} %bitcast.95) | data formatting | bytes 12845056 | tf_op jit(solution)/shard_map/reshape | solution.py:514
  165.2 1.7 %copy.28 = f32[896,896]{1,0:T(8,128)} copy(f32[896,896]{1,0:T(8,128)S(1)} %copy-done.1) | data formatting | bytes 6422528
  (2 shorter events, 0.0 us)
Async XLA Ops:
  69.7 2.0 %copy-start = (bf16[8,4,16,3584]{3,2,1,0:T(8,128)(2,1)S(1)}, bf16[8,4,16,3584]{3,2,1,0:T(8,128)(2,1)}, u32[]{:S(2)}) copy-start(bf16[8,4,16,3584]{3,2,1,0:T(8,128)(2,1)} %get-tuple-element.8) | copy-start | bytes 11010052
  158.9 6.3 %copy-start.1 = (f32[896,896]{1,0:T(8,128)S(1)}, f32[896,896]{1,0:T(8,128)}, u32[]{:S(2)}) copy-start(f32[896,896]{1,0:T(8,128)} %get-tuple-element.19) | copy-start | bytes 9633796

commit v5 on v4

--- a/solution.py
+++ b/solution.py
@@ -302,15 +302,18 @@
 
 
 def server_kernel(
-    cohorts, gain, high, low, tokens, base, momentum, now, prev,
-    all_ref, momentum_ref, fresh, got, to_far, to_pair, kept,
+    cohorts, gain, errors, factors, tokens, weights, momentum, now, prev,
+    all_ref, momentum_ref, fresh, base, fetched, got, to_far, to_pair, kept,
 ):
     lines = fresh.shape[1]
 
     def produce(piece):
         here = pl.ds(pl.multiple_of(piece * lines, lines), lines)
+        scaled = errors[:, here].astype(jnp.float32) * factors[...]
+        high = scaled.astype(jnp.bfloat16)
+        low = (scaled - high.astype(jnp.float32)).astype(jnp.bfloat16)
         both = lax.dot_general(
-            jnp.concatenate([high[:, here], low[:, here]], axis=1),
+            jnp.concatenate([high, low], axis=1),
             tokens[...],
             (((0,), (0,)), ((), ())),
             preferred_element_type=jnp.float32,
@@ -327,25 +330,33 @@
             (base[here].astype(jnp.float32) + SERVER_LR * new_momentum).astype(fresh.dtype)[None]
         )
 
+    width = base.shape[1]
+    start = pl.multiple_of(lax.axis_index("cohort") * width, 128)
+    fetch = pltpu.make_async_copy(weights.at[:, pl.ds(start, width)], base, fetched)
+    fetch.start()
     greet(cohorts, lax.axis_index("cohort"), lax.axis_index("fsdp"), [])
+    fetch.wait()
     spread_kernel(cohorts, fresh, all_ref, got, to_far, to_pair, kept, produce=produce)
 
 
-def serve(high, low, tokens, base, momentum, now, prev, gain, cohorts):
-    hidden, width = base.shape
+def serve(errors, factors, tokens, weights, momentum, now, prev, gain, cohorts):
+    hidden, width = momentum.shape
     lines = math.gcd(hidden, 128)
     pieces = hidden // lines
+    factors = jnp.broadcast_to(factors, errors.shape[:-1] + (lines,)).reshape(-1, lines)
     return pl.pallas_call(
         lambda *refs: server_kernel(cohorts, gain, *refs),
         name="serve",
         out_shape=(
-            jax.ShapeDtypeStruct((cohorts, pieces, lines, width), base.dtype),
+            jax.ShapeDtypeStruct((cohorts, pieces, lines, width), weights.dtype),
             jax.ShapeDtypeStruct(momentum.shape, momentum.dtype),
         ),
-        in_specs=[IN_VMEM] * 7,
+        in_specs=[IN_VMEM] * 3 + [ANY] + [IN_VMEM] * 3,
         out_specs=(ANY, IN_VMEM),
         scratch_shapes=[
-            pltpu.VMEM((pieces, lines, width), base.dtype),
+            pltpu.VMEM((pieces, lines, width), weights.dtype),
+            pltpu.VMEM((hidden, width), weights.dtype),
+            DMA,
             DMA((cohorts, pieces)),
             DMA((max(cohorts // 2 - 1, 1), pieces)),
             DMA((cohorts, pieces)),
@@ -354,7 +365,7 @@
         compiler_params=pltpu.CompilerParams(
             collective_id=2, has_side_effects=True, vmem_limit_bytes=60 << 20
         ),
-    )(high, low, tokens, base, momentum, now, prev)
+    )(errors.reshape(-1, hidden), factors, tokens, weights, momentum, now, prev)
 
 
 def errors_kernel(
@@ -494,16 +505,13 @@
     errors, squared = spread_errors(errors.reshape(shards, -1, hidden), squared, cohorts, shards)
     factors = -rate * clip_factor(squared[:, :, 0])
     errors = errors.reshape(cohorts, shards, clients, steps * count, hidden)
-    high, low = split_scaled(errors, factors[:, None, :, None, None])
     owner_width = columns.shape[-1]
-    owner_start = lax.axis_index("cohort") * owner_width
-    base_part = lax.dynamic_slice_in_dim(weights, owner_start, owner_width, 1)
     gain = math.sqrt(hidden * shards * depth) / (cohorts * clients * CLIP_BOUND)
     blocks, new_momentum = serve(
-        high,
-        low,
+        errors,
+        factors[:, None, :, None, None],
         columns.reshape(-1, owner_width),
-        base_part,
+        weights,
         momentum,
         noise_now,
         noise_prev,

time: 167 us -> 160 us (0.958)
  other arithmetic: 6.7 us -> 1.59 us
    convert_element_type x1 -> x0, other arithmetic: 5.11 us -> none  [split_scaled(): low = (scaled - high.astype(jnp.float32)).astype(jnp.bfloat16)]
    dynamic_slice x1 -> x0, local copies, waits for them, and re-layouts: 2.71 us -> none  [factor_body(): base_part = lax.dynamic_slice_in_dim(weights, owner_start, owner_width, 1)]
where the time goes in v5:
time: 160 us
  Pallas kernels  132 us (82%)
  local copies, waits for them, and re-layouts  14 us (9%)
  matrix products  12 us (8%)
    pallas_call x1, Pallas kernels, gather_tokens(): pl.pallas_call(lambda *refs: gather_kernel(cohorts, shards, *refs), name=...  56 us
    pallas_call x1, Pallas kernels, serve(): pl.pallas_call(lambda *refs: server_kernel(cohorts, gain, *refs), name='s...  48.3 us
    pallas_call x1, Pallas kernels, spread_errors(): pl.pallas_call(lambda *refs: errors_kernel(cohorts, shards, *refs), name=...  27.1 us
    dot_general x1, matrix products, products_of(): lax.dot_general(tokens, weights, (((1,), (1,)), ((), ())), preferred_elem...  9.09 us
    reshape x1, local copies, waits for them, and re-layouts, factor_body(): new_weights = blocks.transpose(1, 0, 2).reshape(hidden, depth)  6.29 us
    unnamed x6, local copies, waits for them, and re-layouts  4.12 us

profile of v5, /device:TPU:0, one launch (start us, length us, event | category | flops | bytes accessed | tf_op | source)
XLA Modules:
  0.0 159.8 jit_solution(5025784866282345266)
XLA Ops:
  0.6 1.3 copy.26
  1.9 56.0 %gather_tokens.1 = (bf16[8,4,16,3584]{3,2,1,0:T(8,128)(2,1)}, bf16[4,8,4,16,896]{4,3,2,1,0:T(8,128)(2,1)}) custom-call(bf16[4,16,3584]{2,1,0:T(8,128)(2,1)} %bitcast.100), custom_call_target="tpu_custom_call" | custom-call | tf_op jit(solution)/shard_map/gather_tokens/pallas_call | solution.py:215
  57.9 9.1 %fusion.3 = f32[4,2,8,8,896]{4,3,1,0,2:T(8,128)S(1)} fusion(bf16[896,3584]{1,0:T(8,128)(2,1)} %refs_3_.1, bf16[8,4,16,3584]{3,2,1,0:T(8,128)(2,1)} %get-tuple-element.8), kind=kOutput, calls=%fused_computation.4 | convolution fusion | flops 3288334336 | bytes 11927552 | tf_op jit(solution)/shard_map/dot_general | solution.py:485
  67.0 0.0 copy-start
  67.0 0.1 copy.25
  67.2 0.7 fusion.17
  67.9 1.2 copy-done
  69.1 0.3 copy.16
  69.4 1.1 fusion.23
  70.5 1.2 fusion.15
  71.8 0.5 fusion.9
  72.3 0.1 pad_maximum_fusion
  72.4 1.0 copy.17
  73.4 0.6 broadcast_in_dim.16.refs_1_
  74.0 27.1 %spread_errors.1 = (bf16[4,8,64,896]{3,2,1,0:T(8,128)(2,1)}, f32[4,4,128]{2,1,0:T(4,128)}) custom-call(bf16[8,64,896]{2,1,0:T(8,128)(2,1)} %bitcast.94, f32[4,128]{1,0:T(4,128)} %broadcast_in_dim.16.refs_1_), custom_call_target="tpu_custom_call" | custom-call | tf_op jit(solution)/shard_map/spread_errors/pallas_call | solution.py:418
  101.2 0.8 multiply_reduce_fusion
  102.0 0.1 broadcast_in_dim.17
  102.1 0.1 broadcast_in_dim.18
  102.2 1.3 broadcast_in_dim.19.refs_1_
  103.5 48.3 %serve.1 = (bf16[4,7,128,896]{3,2,1,0:T(8,128)(2,1)}, f32[896,896]{1,0:T(8,128)}) custom-call(bf16[2048,896]{1,0:T(8,128)(2,1)} %bitcast.97, f32[2048,128]{1,0:T(8,128)} %broadcast_in_dim.19.refs_1_, bf16[2048,896]{1,0:T(8,128)(2,1)} %bitcast.96, bf16[896,3584]{1,0:T(8,128)(2,1)} %refs_3_.1, f32[896,896]{1,0:T(8,128)} %refs_4_.1, bf16[896,896]{1,0:T(8,128)(2,1)} %refs_5_.1, ...), custom_call_target="tpu_custom_call" | custom-call | tf_op jit(solution)/shard_map/serve/pallas_call | solution.py:347
  151.8 0.0 copy-start.1
  151.8 6.3 %copy.22 = bf16[4,112,8,896]{3,2,0,1:T(8,128)(2,1)} copy(bf16[4,112,8,896]{3,2,1,0:T(8,128)(2,1)} %bitcast.90) | data formatting | bytes 12845056 | tf_op jit(solution)/shard_map/reshape | solution.py:522
  158.1 0.0 copy-done.1
  158.1 1.7 %copy.28 = f32[896,896]{1,0:T(8,128)} copy(f32[896,896]{1,0:T(8,128)S(1)} %copy-done.1) | data formatting | bytes 6422528
  (1 shorter events, 0.0 us)
Async XLA Ops:
  67.0 2.0 %copy-start = (bf16[8,4,16,3584]{3,2,1,0:T(8,128)(2,1)S(1)}, bf16[8,4,16,3584]{3,2,1,0:T(8,128)(2,1)}, u32[]{:S(2)}) copy-start(bf16[8,4,16,3584]{3,2,1,0:T(8,128)(2,1)} %get-tuple-element.8) | copy-start | bytes 11010052
  151.8 6.3 %copy-start.1 = (f32[896,896]{1,0:T(8,128)S(1)}, f32[896,896]{1,0:T(8,128)}, u32[]{:S(2)}) copy-start(f32[896,896]{1,0:T(8,128)} %get-tuple-element.17) | copy-start | bytes 9633796
